TPU v7x, 256 devices: a whole 4x4x8 slice. The times are simulated.
256 devices in a mesh: chan: 8 (over y_hi, x), win: 32 (over y_lo, z, core).
Axes of the slice: x: 4, y: 4 (y_hi: 2, y_lo: 2; y = y_hi * 2 + y_lo), z: 8, core: 2. Of those that a mesh axis runs over, the one named last changes fastest.
Arguments:
- raw: bfloat16 [128, 3200, 1024], P('win', None, 'chan'), may hold values from -6 to 6
- offsets: int32 [128], P('win'), may hold values from 0 to 128
- quality: int32 [128, 1024], P('win', 'chan'), may hold values 0 or 1
Outputs:
- stack: bfloat16 [384, 2, 1024, 1024], P('win', None, 'chan')
All inputs are finite; a program needn't handle non-finite values. No bound on the sum of `quality` on one device may be relied on, other than what follows from the above.
Results may differ from a plain program's by a relative error of at most 0.0064.
Values may be sent and summed in bfloat16 or wider, within the bound.
A program may use at most 64 MiB of HBM per device.

v0:
```python
import math

import jax
import jax.numpy as jnp
from jax import lax
from jax.sharding import PartitionSpec as P

F = 384
L = 3072
FIRST_BIN = 60


epsilon = 1e-05


def dft_table():
    sample_idx = jnp.arange(L, dtype=jnp.int32)
    bin_idx = FIRST_BIN + jnp.arange(F, dtype=jnp.int32)
    residue = bin_idx[:, None] * sample_idx[None, :] % L
    angles = residue.astype(jnp.float32) * (2.0 * math.pi / L)
    return jnp.concatenate([jnp.cos(angles), -jnp.sin(angles)], 0).astype(jnp.bfloat16)


def cross_spectra(mine, partner):
    stack_scale = 1.0 / math.sqrt(mine.shape[0])
    real_mine = mine[:, 0]
    imag_mine = mine[:, 1]
    real_other = partner[:, 0]
    imag_other = partner[:, 1]
    real_part = jnp.einsum(
        "wfi,wfj->fij", real_mine, real_other, preferred_element_type=jnp.float32
    )
    real_part = real_part + jnp.einsum(
        "wfi,wfj->fij", imag_mine, imag_other, preferred_element_type=jnp.float32
    )
    imag_part = jnp.einsum(
        "wfi,wfj->fij", imag_mine, real_other, preferred_element_type=jnp.float32
    )
    imag_part = imag_part - jnp.einsum(
        "wfi,wfj->fij", real_mine, imag_other, preferred_element_type=jnp.float32
    )
    return (jnp.stack([real_part, imag_part], 1) * stack_scale).astype(jnp.bfloat16)


def local(raw, offsets, quality):
    table = dft_table()

    def cut_window(segment, shift_at):
        return lax.dynamic_slice_in_dim(segment, shift_at, L, 0)

    windows = jax.vmap(cut_window)(raw, offsets)
    transform = jnp.einsum("kl,wlc->wkc", table, windows, preferred_element_type=jnp.float32)
    band_power = jnp.sum(transform * transform, axis=1, keepdims=True) / F
    whiten = lax.rsqrt(band_power + epsilon) * quality.astype(jnp.float32)[:, None, :]
    block_width = raw.shape[2]
    spectra = (transform * whiten).astype(jnp.bfloat16).reshape(raw.shape[0], 2, F, block_width)
    gathered = lax.all_gather(spectra, "chan", axis=3, tiled=True)
    by_bin = lax.all_to_all(gathered, "win", split_axis=2, concat_axis=0, tiled=True)
    mine = lax.dynamic_slice_in_dim(by_bin, lax.axis_index("chan") * block_width, block_width, 3)
    return cross_spectra(mine, by_bin)


def solution(mesh):
    in_specs = (P("win", None, "chan"), P("win"), P("win", "chan"))
    out_specs = P("win", None, "chan", None)
    return jax.shard_map(local, mesh=mesh, in_specs=in_specs, out_specs=out_specs, check_vma=False)
```

profile of v0, /device:TPU:32, one launch (start us, length us, event | category | flops | bytes accessed | tf_op | source)
XLA Modules:
  0.0 390.3 jit_solution(9089974725493236142)
XLA Ops:
  6.5 0.0 all-gather.2.cloned.1.call-start
  6.5 0.7 fusion.14
  7.2 0.1 copy.21
  7.3 13.5 %while.1 = (s32[]{:T(128)}, bf16[4,3200,128]{2,1,0:T(8,128)(2,1)}, s32[4,3]{1,0:T(4,128)S(1)}, bf16[4,3072,128]{2,1,0:T(8,128)(2,1)S(1)}, s32[]{:T(128)}) while((s32[]{:T(128)}, bf16[4,3200,128]{2,1,0:T(8,128)(2,1)}, s32[4,3]{1,0:T(4,128)S(1)}, bf16[4,3072,128]{2,1,0:T(8,128)(2,1)S(1)}, s32[]{:T(128)}) %tuple.24), condition=%wide.while_cond, body=%wide.while_body.sunk | while | flops 2 | bytes 1572989 | solution.py:49
  7.3 0.7 fusion.23
  8.0 2.7 dynamic-slice_dynamic-update-slice_fusion.2
  10.7 0.7 fusion.23
  11.4 2.7 dynamic-slice_dynamic-update-slice_fusion.2
  14.1 0.7 fusion.23
  14.7 2.7 dynamic-slice_dynamic-update-slice_fusion.2
  17.5 0.7 fusion.23
  18.1 2.7 dynamic-slice_dynamic-update-slice_fusion.2
  20.8 20.3 %cosine_convert_fusion = (bf16[384,3072]{1,0:T(8,128)(2,1)S(1)}, bf16[384,3072]{1,0:T(8,128)(2,1)S(1)}) fusion(s32[384]{0:T(512)S(1)} %iota_add_fusion), kind=kLoop, calls=%fused_computation.14 | loop fusion | flops 14155776 | bytes 4720128 | tf_op jit(solution)/shard_map/convert
  41.1 0.0 copy-start.1
  41.1 2.8 multiply_reduce_fusion
  43.9 0.0 copy-done.1
  43.9 0.2 fusion.13
  44.1 0.2 reshape.12
  44.3 2.1 copy.23
  46.3 0.0 all-gather.2.cloned.1.call-update
  46.4 160.2 %all-gather.2.cloned.1.call-done = bf16[4,2,384,1024]{3,1,0,2:T(2,128)(2,1)} async-done(((bf16[4,2,384,128]{3,1,0,2:T(2,128)(2,1)}), bf16[4,2,384,1024]{3,1,0,2:T(2,128)(2,1)}) %all-gather.2.cloned.1.call-update) | async-done | bytes 6291472 | tf_op jit(solution)/shard_map/all_gather | solution.py:57
  206.6 7.7 %all-to-all-start = ((bf16[4,2,384,1024]{3,1,0,2:T(2,128)(2,1)}), bf16[4,2,384,1024]{3,1,0,2:T(2,128)(2,1)}, u32[]{:S(2)}, u32[]{:S(2)}) async-start(bf16[4,2,384,1024]{3,1,0,2:T(2,128)(2,1)} %all-gather.2.cloned.1.call-done), calls=%async_computation | async-start | bytes 12582912 | tf_op jit(solution)/shard_map/all_to_all | solution.py:58
  214.3 138.2 %all-to-all-done = bf16[4,2,384,1024]{3,1,0,2:T(2,128)(2,1)} async-done(((bf16[4,2,384,1024]{3,1,0,2:T(2,128)(2,1)}), bf16[4,2,384,1024]{3,1,0,2:T(2,128)(2,1)}, u32[]{:S(2)}, u32[]{:S(2)}) %all-to-all-start) | async-done | bytes 6291488 | tf_op jit(solution)/shard_map/all_to_all | solution.py:58
  352.5 8.8 %copy.25 = bf16[32,4,2,12,1024]{4,1,0,3,2:T(4,128)(2,1)} copy(bf16[32,4,2,12,1024]{4,2,1,3,0:T(2,128)(2,1)} %bitcast.5) | data formatting | bytes 12582912 | tf_op jit(solution)/shard_map/all_to_all | solution.py:58
  361.3 9.7 %all_to_all.16 = bf16[128,2,12,1024]{3,0,2,1:T(8,128)(2,1)} reshape(bf16[32,4,2,12,1024]{4,1,0,3,2:T(4,128)(2,1)} %copy.25) | data formatting | bytes 12582912 | tf_op jit(solution)/shard_map/all_to_all | solution.py:58
  371.0 3.2 fusion.10
  374.2 0.7 copy-done
  374.8 1.0 fusion.9
  375.9 1.0 add_bitcast_fusion
  376.9 1.0 subtract_bitcast_fusion
  378.0 1.9 fusion
  379.9 3.5 copy.30
  (10 shorter events, 0.1 us)
Async XLA Ops:
  6.5 200.0 %all-gather.2.cloned.1.call-start = ((), (), s32[]{:S(2)}) async-start(), calls=%async_computation.1 | async-start | bytes 7077888 | tf_op jit(solution)/shard_map/all_gather | solution.py:57
  41.1 2.8 copy-start.1
  206.6 146.0 %all-to-all-start = ((bf16[4,2,384,1024]{3,1,0,2:T(2,128)(2,1)}), bf16[4,2,384,1024]{3,1,0,2:T(2,128)(2,1)}, u32[]{:S(2)}, u32[]{:S(2)}) async-start(bf16[4,2,384,1024]{3,1,0,2:T(2,128)(2,1)} %all-gather.2.cloned.1.call-done), calls=%async_computation | async-start | bytes 12582912 | tf_op jit(solution)/shard_map/all_to_all | solution.py:58
  371.0 3.9 copy-start
Sparse Core Ops, SparseCore 0:
  46.5 160.0 all-gather.1
where the time goes:
time: 394 us; the launch traced here: 390 us
  waiting for transfers between devices  298 us (76%)
  local copies, waits for them, and re-layouts  38.4 us (10%)
  other arithmetic  23 us (6%)
  between operations  13.5 us (3%)
  matrix products  9.09 us (2%)
  starting transfers between devices  7.72 us (2%)
    all_gather x1, waiting for transfers between devices, local(): gathered = lax.all_gather(spectra, 'chan', axis=3, tiled=True)  160 us
    all_to_all x1, waiting for transfers between devices, local(): lax.all_to_all(gathered, 'win', split_axis=2, concat_axis=0, tiled=True)  138 us
    another operation x1, other arithmetic  20.3 us
    all_to_all x2, local copies, waits for them, and re-layouts, local(): lax.all_to_all(gathered, 'win', split_axis=2, concat_axis=0, tiled=True)  18.4 us
    gather x12, local copies, waits for them, and re-layouts  13.4 us
  transfers between devices with their start and end apart: 2, of which 2 were waited for; matrix products, arithmetic and copies ran while one was open for 0% of the time, Pallas kernels for 0%

commit v1 on v0

--- a/solution.py
+++ b/solution.py
@@ -54,9 +54,8 @@
     whiten = lax.rsqrt(band_power + epsilon) * quality.astype(jnp.float32)[:, None, :]
     block_width = raw.shape[2]
     spectra = (transform * whiten).astype(jnp.bfloat16).reshape(raw.shape[0], 2, F, block_width)
-    gathered = lax.all_gather(spectra, "chan", axis=3, tiled=True)
-    by_bin = lax.all_to_all(gathered, "win", split_axis=2, concat_axis=0, tiled=True)
-    mine = lax.dynamic_slice_in_dim(by_bin, lax.axis_index("chan") * block_width, block_width, 3)
+    mine = lax.all_to_all(spectra, "win", split_axis=2, concat_axis=0, tiled=True)
+    by_bin = lax.all_gather(mine, "chan", axis=3, tiled=True)
     return cross_spectra(mine, by_bin)
 
 

time: 394 us -> 199 us (0.51)
  waiting for transfers between devices: 298 us -> 101 us
  blocking collectives: 0 us -> 32.9 us
  local copies, waits for them, and re-layouts: 38.4 us -> 19.9 us
  starting transfers between devices: 7.72 us -> 0.01 us
    all_to_all x1 -> x0, waiting for transfers between devices: 138 us -> none  [local(): lax.all_to_all(gathered, 'win', split_axis=2, concat_axis=0, tiled=True)]
    all_gather x1, waiting for transfers between devices: 160 us -> 101 us  [local(): by_bin = lax.all_gather(mine, 'chan', axis=3, tiled=True)]
    all_to_all x0 -> x1, blocking collectives: none -> 32.9 us  [local(): lax.all_to_all(spectra, 'win', split_axis=2, concat_axis=0, tiled=True)]
    all_to_all x2 -> x1, local copies, waits for them, and re-layouts: 18.4 us -> 1.23 us  [local(): lax.all_to_all(spectra, 'win', split_axis=2, concat_axis=0, tiled=True)]
    all_to_all x1 -> x0, starting transfers between devices: 7.72 us -> none  [local(): lax.all_to_all(gathered, 'win', split_axis=2, concat_axis=0, tiled=True)]
  transfers between devices with their start and end apart: 2 -> 1, of which waited for: 2 -> 1; matrix products, arithmetic and copies ran while one was open for 0% -> 0% of each run, Pallas kernels for 0% -> 0%
where the time goes in v1:
time: 199 us
  waiting for transfers between devices  101 us (51%)
  blocking collectives  32.9 us (17%)
  other arithmetic  23 us (12%)
  local copies, waits for them, and re-layouts  19.9 us (10%)
  between operations  13.5 us (7%)
  matrix products  9.06 us (5%)
    all_gather x1, waiting for transfers between devices, local(): by_bin = lax.all_gather(mine, 'chan', axis=3, tiled=True)  101 us
    all_to_all x1, blocking collectives, local(): lax.all_to_all(spectra, 'win', split_axis=2, concat_axis=0, tiled=True)  32.9 us
    another operation x1, other arithmetic  20.3 us
    gather x12, local copies, waits for them, and re-layouts  12.9 us
  transfers between devices with their start and end apart: 1, of which 1 were waited for; matrix products, arithmetic and copies ran while one was open for 0% of the time, Pallas kernels for 0%

profile of v1, /device:TPU:32, one launch (start us, length us, event | category | flops | bytes accessed | tf_op | source)
XLA Modules:
  0.0 199.0 jit_solution(6560308641841576930)
XLA Ops:
  6.5 0.0 all-gather.2.cloned.1.call-start
  6.5 0.7 fusion.14
  7.2 0.1 copy.21
  7.3 12.9 %while.1 = (s32[]{:T(128)}, bf16[4,3200,128]{2,1,0:T(8,128)(2,1)}, s32[4,3]{1,0:T(4,128)S(1)}, bf16[4,3072,128]{2,1,0:T(8,128)(2,1)S(1)}, s32[]{:T(128)}) while((s32[]{:T(128)}, bf16[4,3200,128]{2,1,0:T(8,128)(2,1)}, s32[4,3]{1,0:T(4,128)S(1)}, bf16[4,3072,128]{2,1,0:T(8,128)(2,1)S(1)}, s32[]{:T(128)}) %tuple.24), condition=%wide.while_cond, body=%wide.while_body.sunk | while | flops 2 | bytes 1572989 | solution.py:49
  7.3 0.6 fusion.19
  7.9 2.6 %dynamic-slice_dynamic-update-slice_fusion.2 = bf16[4,3072,128]{2,1,0:T(8,128)(2,1)S(1)} fusion(bf16[4,3072,128]{2,1,0:T(8,128)(2,1)S(1)} %get-tuple-element.76, s32[]{:T(128)S(6)} %copy.40, bf16[4,3200,128]{2,1,0:T(8,128)(2,1)} %get-tuple-element.79, s32[]{:T(128)} %bitcast.44, s32[]{:T(128)} %bitcast.45), kind=kLoop, calls=%fused_computation.clone.1 | loop fusion | bytes 1572876 | tf_op jit(solution)/shard_map/vmap()/gather
  10.6 0.6 fusion.19
  11.1 2.6 %dynamic-slice_dynamic-update-slice_fusion.2 = bf16[4,3072,128]{2,1,0:T(8,128)(2,1)S(1)} fusion(bf16[4,3072,128]{2,1,0:T(8,128)(2,1)S(1)} %get-tuple-element.76, s32[]{:T(128)S(6)} %copy.40, bf16[4,3200,128]{2,1,0:T(8,128)(2,1)} %get-tuple-element.79, s32[]{:T(128)} %bitcast.44, s32[]{:T(128)} %bitcast.45), kind=kLoop, calls=%fused_computation.clone.1 | loop fusion | bytes 1572876 | tf_op jit(solution)/shard_map/vmap()/gather
  13.8 0.6 fusion.19
  14.4 2.6 %dynamic-slice_dynamic-update-slice_fusion.2 = bf16[4,3072,128]{2,1,0:T(8,128)(2,1)S(1)} fusion(bf16[4,3072,128]{2,1,0:T(8,128)(2,1)S(1)} %get-tuple-element.76, s32[]{:T(128)S(6)} %copy.40, bf16[4,3200,128]{2,1,0:T(8,128)(2,1)} %get-tuple-element.79, s32[]{:T(128)} %bitcast.44, s32[]{:T(128)} %bitcast.45), kind=kLoop, calls=%fused_computation.clone.1 | loop fusion | bytes 1572876 | tf_op jit(solution)/shard_map/vmap()/gather
  17.0 0.6 fusion.19
  17.6 2.6 %dynamic-slice_dynamic-update-slice_fusion.2 = bf16[4,3072,128]{2,1,0:T(8,128)(2,1)S(1)} fusion(bf16[4,3072,128]{2,1,0:T(8,128)(2,1)S(1)} %get-tuple-element.76, s32[]{:T(128)S(6)} %copy.40, bf16[4,3200,128]{2,1,0:T(8,128)(2,1)} %get-tuple-element.79, s32[]{:T(128)} %bitcast.44, s32[]{:T(128)} %bitcast.45), kind=kLoop, calls=%fused_computation.clone.1 | loop fusion | bytes 1572876 | tf_op jit(solution)/shard_map/vmap()/gather
  20.3 20.3 %cosine_convert_fusion = (bf16[384,3072]{1,0:T(8,128)(2,1)S(1)}, bf16[384,3072]{1,0:T(8,128)(2,1)S(1)}) fusion(s32[384]{0:T(512)S(1)} %iota_add_fusion), kind=kLoop, calls=%fused_computation.14 | loop fusion | flops 14155776 | bytes 4720128 | tf_op jit(solution)/shard_map/convert
  40.5 0.0 copy-start.2
  40.5 2.8 %multiply_reduce_fusion = (f32[4,128]{1,0:T(4,128)S(1)}, f32[4,128,768]{2,1,0:T(8,128)S(1)}) fusion(bf16[4,3072,128]{2,1,0:T(8,128)(2,1)S(1)} %get-tuple-element.12, bf16[384,3072]{1,0:T(8,128)(2,1)S(1)} %get-tuple-element.36, bf16[384,3072]{1,0:T(8,128)(2,1)S(1)} %get-tuple-element.35), kind=kOutput, calls=%fused_computation.26 | convolution fusion | flops 2426142208 | bytes 9439232 | tf_op jit(solution)/shard_map/kl,wlc->wkc/dot_general | solution.py:52
  43.3 0.0 copy-done.2
  43.4 0.2 fusion.13
  43.5 0.2 reshape.12
  43.7 1.3 copy.23
  45.1 32.9 %all_to_all.18 = bf16[4,2,384,128]{3,1,0,2:T(2,128)(2,1)S(1)} all-to-all(bf16[4,2,384,128]{3,1,0,2:T(2,128)(2,1)S(1)} %copy.23), channel_id=1, replica_groups=mesh['chan'=8,'win'=32] {'win'}, dimensions={2} | all-to-all | bytes 1572864 | tf_op jit(solution)/shard_map/all_to_all | solution.py:57
  77.9 1.2 copy.25
  79.2 0.0 all-gather.2.cloned.1.call-update
  79.2 0.0 copy-start.1
  79.2 100.5 %all-gather.2.cloned.1.call-done = bf16[128,2,12,1024]{3,0,2,1:T(8,128)(2,1)} async-done(((bf16[128,2,12,128]{3,0,2,1:T(8,128)(2,1)}), bf16[128,2,12,1024]{3,0,2,1:T(8,128)(2,1)}) %all-gather.2.cloned.1.call-update) | async-done | bytes 6291472 | tf_op jit(solution)/shard_map/all_gather | solution.py:58
  179.7 3.2 %fusion.9 = f32[12,128,1024]{2,1,0:T(8,128)S(1)} fusion(bf16[128,2,12,1024]{3,0,2,1:T(8,128)(2,1)} %all-gather.2.cloned.1.call-done, bf16[128,2,12,128]{3,0,2,1:T(8,128)(2,1)} %bitcast.47), kind=kOutput, calls=%fused_computation.21 | convolution fusion | flops 402653184 | bytes 9830400 | tf_op jit(solution)/shard_map/wfi,wfj->fij/dot_general | solution.py:36
  182.9 0.0 copy-done.1
  182.9 0.7 copy-done
  183.6 1.0 fusion.10
  184.6 1.0 subtract_bitcast_fusion
  185.6 1.0 add_bitcast_fusion
  186.7 1.9 fusion
  188.6 3.5 %copy.30 = bf16[12,2,128,1024]{3,2,1,0:T(8,128)(2,1)} copy(bf16[12,2,128,1024]{3,2,0,1:T(8,128)(2,1)S(1)} %fusion) | data formatting | bytes 12582912 | tf_op jit(solution)/shard_map/convert_element_type | solution.py:42
  (10 shorter events, 0.1 us)
Async XLA Ops:
  6.5 173.2 %all-gather.2.cloned.1.call-start = ((), (), s32[]{:S(2)}) async-start(), calls=%async_computation.1 | async-start | bytes 7077888 | tf_op jit(solution)/shard_map/all_gather | solution.py:58
  40.5 2.8 %copy-start.2 = (s32[4,128]{1,0:T(4,128)S(1)}, s32[4,128]{1,0:T(4,128)}, u32[]{:S(2)}) copy-start(s32[4,128]{1,0:T(4,128)} %param.5) | copy-start | bytes 6148
  79.2 103.7 %copy-start.1 = (bf16[32,4,2,12,128]{4,1,0,3,2:T(4,128)(2,1)S(1)}, bf16[32,4,2,12,128]{4,1,0,3,2:T(4,128)(2,1)}, u32[]{:S(2)}) copy-start(bf16[32,4,2,12,128]{4,1,0,3,2:T(4,128)(2,1)} %copy.25) | copy-start | bytes 2359300
  179.7 3.8 %copy-start = (bf16[128,2,12,1024]{3,0,2,1:T(8,128)(2,1)S(1)}, bf16[128,2,12,1024]{3,0,2,1:T(8,128)(2,1)}, u32[]{:S(2)}) copy-start(bf16[128,2,12,1024]{3,0,2,1:T(8,128)(2,1)} %all-gather.2.cloned.1.call-done) | copy-start | bytes 18874372
Sparse Core Ops, SparseCore 0:
  79.3 100.3 all-gather.1

commit v2 on v1

v2 whole, which is shorter than its diff:
```python
import math

import jax
import jax.numpy as jnp
import numpy as np
from jax import lax
from jax.experimental import pallas as pl
from jax.experimental.pallas import tpu as pltpu
from jax.sharding import PartitionSpec as P

C = 1024
F = 384
L = 3072
FIRST_BIN = 60
WINDOWS = 128
SEG = 3200
EPSILON = 1e-05

LANES = 128
LOCAL_W = 4
BINS = 12
X_SIZE, Y_SIZE, Z_SIZE = 4, 4, 8
COLUMN = 2 * Z_SIZE
CHAN, WIN = 8, 32
GROUPS = 6
GROUP_BINS = BINS // GROUPS
MESH = pl.DeviceIdType.MESH


def table_seeds():
    bins = FIRST_BIN + np.arange(F, dtype=np.int64)
    first = 2.0 * math.pi / L * (bins[:, None] * np.arange(LANES)[None, :] % L)
    turn = 2.0 * math.pi / L * (bins * LANES % L)
    turn = np.broadcast_to(turn[:, None], (F, LANES))
    return [a.astype(np.float32) for a in (np.cos(first), -np.sin(first), np.cos(turn), -np.sin(turn))]


def spectra_kernel(off_ref, quality_ref, cos_ref, msin_ref, tcos_ref, tmsin_ref, raw_ref, out_ref,
                   table, rows, wide, pair, product, mixed, sem):
    copies = [pltpu.make_async_copy(raw_ref.at[w], rows.at[w], sem.at[w]) for w in range(LOCAL_W)]
    for copy in copies:
        copy.start()

    step = 48

    def table_rows(i, carry):
        at = pl.multiple_of(i * step, 16)
        here = pl.ds(at, step)
        below = pl.ds(pl.multiple_of(F + at, 16), step)
        c, m = cos_ref[here, :], msin_ref[here, :]
        tc, tm = tcos_ref[here, :], tmsin_ref[here, :]
        for a in range(L // LANES):
            table[here, a * LANES:(a + 1) * LANES] = c.astype(jnp.bfloat16)
            table[below, a * LANES:(a + 1) * LANES] = m.astype(jnp.bfloat16)
            c, m = c * tc - m * tm, m * tc + c * tm
        return carry

    lax.fori_loop(0, F // step, table_rows, 0)

    for first in range(0, LOCAL_W, 2):
        for half in range(2):
            w = first + half
            copies[w].wait()
            wide[...] = rows[w].astype(jnp.float32)
            pair[:, half * LANES:(half + 1) * LANES] = wide[pl.ds(off_ref[w], L), :].astype(jnp.bfloat16)
        product[...] = jnp.dot(table[...], pair[...], preferred_element_type=jnp.float32)
        power = jnp.sum(product[...] * product[...], axis=0, keepdims=True) / F
        whiten = lax.rsqrt(power + EPSILON)
        for half in range(2):
            w = first + half
            lanes = slice(half * LANES, (half + 1) * LANES)
            gain = whiten[:, lanes] * quality_ref[w:w + 1, :].astype(jnp.float32)
            for p in range(2):
                mixed[pl.ds(p * LOCAL_W + w, F, stride=8), :] = product[p * F:(p + 1) * F, lanes] * gain
    out_ref[...] = mixed[...].astype(jnp.bfloat16)


def whitened_spectra(raw, offsets, quality):
    vmem = pl.BlockSpec(memory_space=pltpu.VMEM)
    return pl.pallas_call(
        spectra_kernel,
        out_shape=jax.ShapeDtypeStruct((F * 8, LANES), jnp.bfloat16),
        in_specs=[pl.BlockSpec(memory_space=pltpu.SMEM)] + [vmem] * 5 + [pl.BlockSpec(memory_space=pl.ANY)],
        out_specs=vmem,
        scratch_shapes=[
            pltpu.VMEM((2 * F, L), jnp.bfloat16),
            pltpu.VMEM((LOCAL_W, SEG, LANES), jnp.bfloat16),
            pltpu.VMEM((SEG, LANES), jnp.float32),
            pltpu.VMEM((L, 2 * LANES), jnp.bfloat16),
            pltpu.VMEM((2 * F, 2 * LANES), jnp.float32),
            pltpu.VMEM((F * 8, LANES), jnp.float32),
            pltpu.SemaphoreType.DMA((LOCAL_W,)),
        ],
        compiler_params=pltpu.CompilerParams(vmem_limit_bytes=40 << 20),
        name="spectra",
    )(offsets, quality, *[jnp.asarray(a) for a in table_seeds()], raw)


def gather_kernel(s_ref, r_ref, t_ref, z_send, y_send, x_send, z_recv, y_recv, x_recv):
    chan, win = lax.axis_index("chan"), lax.axis_index("win")
    y_hi, x = chan // X_SIZE, chan % X_SIZE
    y_lo, spot = win // COLUMN, win % COLUMN
    y = y_hi * 2 + y_lo

    def column(i):
        return chan, y_lo * COLUMN + i

    def at_y(step):
        other = (y + step) % Y_SIZE
        return (other // 2) * X_SIZE + x, (other % 2) * COLUMN + spot

    def at_x(step):
        return y_hi * X_SIZE + (x + step) % X_SIZE, win

    def other_spot(d):
        return (spot + d) % COLUMN

    order = [d for k in range(1, COLUMN // 2) for d in (k, COLUMN - k)] + [COLUMN // 2]
    peers = [column(other_spot(d)) for d in order] + [at_y(1), at_y(3), at_y(2), at_x(1), at_x(3)]
    barrier = pltpu.get_barrier_semaphore()
    for peer in peers:
        pl.semaphore_signal(barrier, inc=1, device_id=peer, device_id_type=MESH)
    pl.semaphore_wait(barrier, len(peers))

    def remote(src, dst, send, recv, peer):
        return pltpu.make_async_remote_copy(
            src_ref=src, dst_ref=dst, send_sem=send, recv_sem=recv, device_id=peer, device_id_type=MESH)

    def bins_of(g):
        return pl.ds(g * GROUP_BINS, GROUP_BINS)

    def z_start(g, carry):
        bins = bins_of(g)
        mine, theirs = r_ref.at[y_hi, x, bins, win], t_ref.at[bins, spot]
        pltpu.make_async_copy(s_ref.at[win, bins], mine, z_recv.at[0, g]).start()
        pltpu.make_async_copy(s_ref.at[(1 - y_lo) * COLUMN + spot, bins], theirs, z_recv.at[1, g]).start()
        for d in order:
            i = other_spot(d)
            remote(s_ref.at[(1 - y_lo) * COLUMN + i, bins], theirs, z_send, z_recv.at[1, g], column(i)).start()
            remote(s_ref.at[y_lo * COLUMN + i, bins], mine, z_send, z_recv.at[0, g], column(i)).start()
        return carry

    lax.fori_loop(0, GROUPS, z_start, 0)

    def whole(ref, sem):
        pltpu.make_async_copy(ref, ref, sem).wait()

    def half(chan_y, chan_x, bins, lo):
        return r_ref.at[chan_y, chan_x, bins, pl.ds(lo * COLUMN, COLUMN)]

    for t in range(GROUPS + 2):
        if t < GROUPS:
            bins = bins_of(t)
            mine = half(y_hi, x, bins, y_lo)
            whole(t_ref.at[bins], z_recv.at[1, t])
            remote(t_ref.at[bins], mine, y_send.at[0], y_recv.at[0, t], at_y(1)).start()
            remote(t_ref.at[bins], mine, y_send.at[1], y_recv.at[1, t], at_y(3)).start()
            whole(mine, z_recv.at[0, t])
            remote(mine, mine, y_send.at[2], y_recv.at[2, t], at_y(2)).start()
        if 0 <= t - 1 < GROUPS:
            g = t - 1
            bins = bins_of(g)
            for k, step in ((0, 3), (1, 1), (2, 2)):
                other = (y + step) % Y_SIZE
                whole(half(other // 2, x, bins, other % 2), y_recv.at[k, g])
            block = r_ref.at[:, x, bins]
            remote(block, block, x_send.at[0], x_recv.at[0, g], at_x(1)).start()
            remote(block, block, x_send.at[1], x_recv.at[1, g], at_x(3)).start()
        if 0 <= t - 2 < GROUPS:
            g = t - 2
            bins = bins_of(g)
            left, right = (x + 3) % X_SIZE, (x + 1) % X_SIZE
            whole(r_ref.at[:, left, bins], x_recv.at[0, g])
            block = r_ref.at[0, left, bins]
            remote(block, block, x_send.at[2], x_recv.at[2, g], at_x(1)).start()
            whole(r_ref.at[:, right, bins], x_recv.at[1, g])
            block = r_ref.at[1, right, bins]
            remote(block, block, x_send.at[3], x_recv.at[3, g], at_x(3)).start()

    far = (x + 2) % X_SIZE
    for g in range(GROUPS):
        for k in range(2):
            whole(r_ref.at[k, far, bins_of(g)], x_recv.at[2 + k, g])
    whole(s_ref.at[pl.ds(0, WIN - 2)], z_send)
    for k in range(2):
        whole(t_ref, y_send.at[k])
        whole(r_ref.at[:, 0], x_send.at[k])
        whole(r_ref.at[0, 0], x_send.at[2 + k])
    whole(r_ref.at[0, 0, :, pl.ds(0, COLUMN)], y_send.at[2])


def gathered_spectra(s):
    return pl.pallas_call(
        gather_kernel,
        out_shape=jax.ShapeDtypeStruct((2, X_SIZE, BINS, WIN, 8, LANES), jnp.bfloat16),
        in_specs=[pl.BlockSpec(memory_space=pltpu.VMEM)],
        out_specs=pl.BlockSpec(memory_space=pl.ANY),
        scratch_shapes=[
            pltpu.VMEM((BINS, COLUMN, 8, LANES), jnp.bfloat16),
            pltpu.SemaphoreType.DMA,
            pltpu.SemaphoreType.DMA((3,)),
            pltpu.SemaphoreType.DMA((4,)),
            pltpu.SemaphoreType.DMA((2, GROUPS)),
            pltpu.SemaphoreType.DMA((3, GROUPS)),
            pltpu.SemaphoreType.DMA((4, GROUPS)),
        ],
        compiler_params=pltpu.CompilerParams(collective_id=0, has_side_effects=True),
        name="gather",
    )(s)


def stack_kernel(chan_ref, r_ref, out_ref):
    own = r_ref[chan_ref[0], 0].astype(jnp.float32)
    turned = pltpu.roll(own.reshape(WIN, 8, LANES), 4, 1)
    row = lax.broadcasted_iota(jnp.int32, (WIN, 8, LANES), 1)
    turned = jnp.where(row < 4, turned, -turned).reshape(WIN * 8, LANES)
    left = jnp.concatenate([own.T, turned.T], 0).astype(jnp.bfloat16)
    scale = 1.0 / math.sqrt(WINDOWS)
    for k in range(0, CHAN, 2):
        right = jnp.concatenate([r_ref[k, 0], r_ref[k + 1, 0]], 1)
        part = jnp.dot(left, right, preferred_element_type=jnp.float32) * scale
        lanes = slice(k * LANES, (k + 2) * LANES)
        out_ref[0, 0, :, lanes] = part[:LANES].astype(jnp.bfloat16)
        out_ref[0, 1, :, lanes] = part[LANES:].astype(jnp.bfloat16)


def stacked(chan, r):
    return pl.pallas_call(
        stack_kernel,
        out_shape=jax.ShapeDtypeStruct((BINS, 2, LANES, C), jnp.bfloat16),
        grid_spec=pltpu.PrefetchScalarGridSpec(
            num_scalar_prefetch=1,
            grid=(BINS,),
            in_specs=[pl.BlockSpec((CHAN, 1, WIN * 8, LANES), lambda f, _: (0, f, 0, 0))],
            out_specs=pl.BlockSpec((1, 2, LANES, C), lambda f, _: (f, 0, 0, 0)),
        ),
        name="stack",
    )(chan, r)


def local(raw, offsets, quality):
    s = whitened_spectra(raw, offsets, quality)
    r = gathered_spectra(s.reshape(WIN, BINS, 8, LANES))
    chan = lax.axis_index("chan").astype(jnp.int32).reshape(1)
    return stacked(chan, r.reshape(CHAN, BINS, WIN * 8, LANES))


def solution(mesh):
    in_specs = (P("win", None, "chan"), P("win"), P("win", "chan"))
    out_specs = P("win", None, "chan", None)
    return jax.shard_map(local, mesh=mesh, in_specs=in_specs, out_specs=out_specs, check_vma=False)
```

time: 199 us -> 103 us (0.52)
  waiting for transfers between devices: 101 us -> 0 us
  Pallas kernels: 0 us -> 94.7 us
  blocking collectives: 32.9 us -> 0 us
  other arithmetic: 23 us -> 0 us
  between operations: 13.5 us -> 0.03 us
  local copies, waits for them, and re-layouts: 19.9 us -> 7.84 us
  matrix products: 9.06 us -> 0 us
    all_gather x1 -> x0, waiting for transfers between devices: 101 us -> none  [local(): by_bin = lax.all_gather(mine, 'chan', axis=3, tiled=True)]
    pallas_call x0 -> x3, Pallas kernels: none -> 94.7 us  [the longest x1 74.7 us: gathered_spectra(): pl.pallas_call(gather_kernel, out_shape=jax.ShapeDtypeStruct((2, X_SIZE,...]
    all_to_all x1 -> x0, blocking collectives: 32.9 us -> none  [local(): lax.all_to_all(spectra, 'win', split_axis=2, concat_axis=0, tiled=True)]
    another operation x1 -> x0, other arithmetic: 20.3 us -> none
    gather x12 -> x0, local copies, waits for them, and re-layouts: 12.9 us -> none
    dot_general x5 -> x0, matrix products: 9.06 us -> none  [the longest x1 3.18 us: cross_spectra(): jnp.einsum('wfi,wfj->fij', imag_mine, real_other, preferred_element_type=...]
    unnamed x8 -> x16, local copies, waits for them, and re-layouts: 0.77 us -> 7.84 us
    convert_element_type x1 -> x0, local copies, waits for them, and re-layouts: 3.51 us -> none  [cross_spectra(): (jnp.stack([real_part, imag_part], 1) * stack_scale).astype(jnp.bfloat16)]
  transfers between devices with their start and end apart: 1 -> 0, of which waited for: 1 -> 0; matrix products, arithmetic and copies ran while one was open for 0% -> 0% of each run, Pallas kernels for 0% -> 0%
where the time goes in v2:
time: 103 us
  Pallas kernels  94.7 us (92%)
  local copies, waits for them, and re-layouts  7.84 us (8%)
    pallas_call x1, Pallas kernels, gathered_spectra(): pl.pallas_call(gather_kernel, out_shape=jax.ShapeDtypeStruct((2, X_SIZE,...  74.7 us
    pallas_call x1, Pallas kernels, stacked(): pl.pallas_call(stack_kernel, out_shape=jax.ShapeDtypeStruct((BINS, 2, LAN...  10.9 us
    pallas_call x1, Pallas kernels, whitened_spectra(): pl.pallas_call(spectra_kernel, out_shape=jax.ShapeDtypeStruct((F * 8, LAN...  9.13 us
    unnamed x16, local copies, waits for them, and re-layouts  7.84 us

profile of v2, /device:TPU:32, one launch (start us, length us, event | category | flops | bytes accessed | tf_op | source)
XLA Modules:
  0.0 102.6 jit_solution(11465227872936457654)
XLA Ops:
  0.0 0.0 copy-start
  0.0 1.9 %copy-done = bf16[4,3200,128]{2,1,0:T(8,128)(2,1)S(1)} copy-done((bf16[4,3200,128]{2,1,0:T(8,128)(2,1)S(1)}, bf16[4,3200,128]{2,1,0:T(8,128)(2,1)}, u32[]{:S(2)}) %copy-start) | copy-done | bytes 3276824
  1.9 0.0 copy-start.2
  1.9 0.9 copy-done.2
  2.9 0.0 copy-start.3
  2.9 0.9 copy-done.3
  3.8 0.0 copy-start.4
  3.8 0.9 copy-done.4
  4.7 0.0 copy-start.5
  4.7 0.9 copy-done.5
  5.6 0.0 copy-start.6
  5.6 0.7 copy-done.6
  6.3 0.0 copy-start.7
  6.3 0.7 copy-done.7
  7.0 9.1 %spectra.1 = bf16[3072,128]{1,0:T(8,128)(2,1)S(1)} custom-call(s32[4]{0:T(128)S(1)} %copy-done.7, s32[4,128]{1,0:T(4,128)S(1)} %copy-done.6, f32[384,128]{1,0:T(8,128)S(1)} %copy-done.5, f32[384,128]{1,0:T(8,128)S(1)} %copy-done.4, f32[384,128]{1,0:T(8,128)S(1)} %copy-done.3, f32[384,128]{1,0:T(8,128)S(1)} %copy-done.2, bf16[4,3200,128]{2,1,0:T(8,128)(2,1)S(1)} %copy-done), custom_call_target="tpu_custom_call" | custom-call | tf_op jit(solution)/shard_map/spectra/pallas_call | solution.py:80
  16.1 0.0 copy-start.1
  16.1 0.9 copy-done.1
  17.0 74.7 %gather.1 = bf16[2,4,12,32,8,128]{5,4,3,2,1,0:T(8,128)(2,1)} custom-call(bf16[32,12,8,128]{3,2,1,0:T(8,128)(2,1)} %bitcast.3), custom_call_target="tpu_custom_call" | custom-call | tf_op jit(solution)/shard_map/gather/pallas_call | solution.py:193
  91.7 10.9 %stack.1 = bf16[12,2,128,1024]{3,2,1,0:T(8,128)(2,1)} custom-call(s32[1]{0:T(128)} %bitcast.chan_ref, bf16[8,12,256,128]{3,2,1,0:T(8,128)(2,1)} %bitcast.4), custom_call_target="tpu_custom_call" | custom-call | tf_op jit(solution)/shard_map/stack/pallas_call | solution.py:228
Async XLA Ops:
  0.0 1.9 %copy-start = (bf16[4,3200,128]{2,1,0:T(8,128)(2,1)S(1)}, bf16[4,3200,128]{2,1,0:T(8,128)(2,1)}, u32[]{:S(2)}) copy-start(bf16[4,3200,128]{2,1,0:T(8,128)(2,1)} %raw_ref.1) | copy-start | bytes 9830404
  1.9 0.9 copy-start.2
  2.9 0.9 copy-start.3
  3.8 0.9 copy-start.4
  4.7 0.9 copy-start.5
  5.6 0.7 copy-start.6
  6.3 0.7 copy-start.7
  16.1 0.9 copy-start.1

commit v3 on v2

v3 whole, which is shorter than its diff:
```python
import math

import jax
import jax.numpy as jnp
import numpy as np
from jax import lax
from jax.experimental import pallas as pl
from jax.experimental.pallas import tpu as pltpu
from jax.sharding import PartitionSpec as P

C = 1024
F = 384
L = 3072
FIRST_BIN = 60
WINDOWS = 128
SEG = 3200
EPSILON = 1e-05

LANES = 128
LOCAL_W = 4
BINS = 12
X_SIZE, Y_SIZE, Z_SIZE = 4, 4, 8
COLUMN = 2 * Z_SIZE
CHAN, WIN = 8, 32
GROUPS = (("y", 0, 1), ("x", 1, 1), ("y", 2, 2), ("x", 4, 2), ("x", 6, 2), ("y", 8, 2), ("y", 10, 1), ("y", 11, 1))
ORDER = (
    ("zy", 0), ("zx", 1), ("uy", 0), ("zy", 2), ("x2x", 1), ("yx", 0),
    ("y1", 1), ("zx", 3), ("uy", 2), ("x2y", 0), ("ux", 1), ("zx", 4),
    ("x2x", 3), ("zy", 5), ("yx", 2), ("ey", 0), ("zy", 6), ("ex", 1),
    ("zy", 7), ("x2x", 4), ("uy", 5), ("y1", 3), ("uy", 6), ("uy", 7),
    ("yx", 5), ("ux", 3), ("x2y", 2), ("y1", 4), ("yx", 6), ("yx", 7),
    ("x2y", 5), ("ex", 3), ("ey", 2), ("ux", 4), ("x2y", 6), ("x2y", 7),
    ("ey", 5), ("ex", 4), ("ey", 6), ("ey", 7),
)
MESH = pl.DeviceIdType.MESH


def table_seeds():
    bins = FIRST_BIN + np.arange(F, dtype=np.int64)
    first = 2.0 * math.pi / L * (bins[:, None] * np.arange(LANES)[None, :] % L)
    turn = 2.0 * math.pi / L * (bins * LANES % L)
    turn = np.broadcast_to(turn[:, None], (F, LANES))
    return np.stack([np.cos(first), -np.sin(first), np.cos(turn), -np.sin(turn)]).astype(np.float32)


def spectra_kernel(off_hbm, quality_hbm, seeds_hbm, raw_hbm, out_ref,
                   off_ref, quality_ref, seeds, table, rows, wide, pair, product, mixed, sem):
    seeds_copy = pltpu.make_async_copy(seeds_hbm, seeds, sem.at[LOCAL_W])
    small = [pltpu.make_async_copy(off_hbm, off_ref, sem.at[LOCAL_W + 1]),
             pltpu.make_async_copy(quality_hbm, quality_ref, sem.at[LOCAL_W + 2])]
    copies = [pltpu.make_async_copy(raw_hbm.at[w], rows.at[w], sem.at[w]) for w in range(LOCAL_W)]
    for copy in [seeds_copy] + small + copies:
        copy.start()
    seeds_copy.wait()

    step = 48

    def table_rows(i, carry):
        at = pl.multiple_of(i * step, 16)
        here = pl.ds(at, step)
        below = pl.ds(pl.multiple_of(F + at, 16), step)
        c, m = seeds[0, here, :], seeds[1, here, :]
        tc, tm = seeds[2, here, :], seeds[3, here, :]
        for a in range(L // LANES):
            table[here, a * LANES:(a + 1) * LANES] = c.astype(jnp.bfloat16)
            table[below, a * LANES:(a + 1) * LANES] = m.astype(jnp.bfloat16)
            c, m = c * tc - m * tm, m * tc + c * tm
        return carry

    lax.fori_loop(0, F // step, table_rows, 0)
    for copy in small:
        copy.wait()

    for first in range(0, LOCAL_W, 2):
        for half in range(2):
            w = first + half
            copies[w].wait()
            wide[half] = rows[w].astype(jnp.float32)
            pair[:, half * LANES:(half + 1) * LANES] = wide[half, pl.ds(off_ref[w], L), :].astype(jnp.bfloat16)
        product[...] = jnp.dot(table[...], pair[...], preferred_element_type=jnp.float32)
        power = jnp.sum(product[...] * product[...], axis=0, keepdims=True) / F
        whiten = lax.rsqrt(power + EPSILON)
        for half in range(2):
            w = first + half
            lanes = slice(half * LANES, (half + 1) * LANES)
            gain = whiten[:, lanes] * quality_ref[w:w + 1, :].astype(jnp.float32)
            for p in range(2):
                mixed[pl.ds(p * LOCAL_W + w, F, stride=8), :] = product[p * F:(p + 1) * F, lanes] * gain
    out_ref[...] = mixed[...].astype(jnp.bfloat16)


def whitened_spectra(raw, offsets, quality):
    anywhere = pl.BlockSpec(memory_space=pl.ANY)
    return pl.pallas_call(
        spectra_kernel,
        out_shape=jax.ShapeDtypeStruct((F * 8, LANES), jnp.bfloat16),
        in_specs=[anywhere] * 4,
        out_specs=pl.BlockSpec(memory_space=pltpu.VMEM),
        scratch_shapes=[
            pltpu.SMEM((LOCAL_W,), jnp.int32),
            pltpu.VMEM((LOCAL_W, LANES), jnp.int32),
            pltpu.VMEM((4, F, LANES), jnp.float32),
            pltpu.VMEM((2 * F, L), jnp.bfloat16),
            pltpu.VMEM((LOCAL_W, SEG, LANES), jnp.bfloat16),
            pltpu.VMEM((2, SEG, LANES), jnp.float32),
            pltpu.VMEM((L, 2 * LANES), jnp.bfloat16),
            pltpu.VMEM((2 * F, 2 * LANES), jnp.float32),
            pltpu.VMEM((F * 8, LANES), jnp.float32),
            pltpu.SemaphoreType.DMA((LOCAL_W + 3,)),
        ],
        compiler_params=pltpu.CompilerParams(vmem_limit_bytes=67043328),
        name="spectra",
    )(offsets, quality, jnp.asarray(table_seeds()), raw)


def gather_kernel(s_ref, r_ref, t_ref, u_ref, z_send, send_sem, z_recv, y_recv, u_recv, x_recv):
    chan, win = lax.axis_index("chan"), lax.axis_index("win")
    y_hi, x = chan // X_SIZE, chan % X_SIZE
    y_lo, spot = win // COLUMN, win % COLUMN
    y = y_hi * 2 + y_lo
    left, right, far = (x + 3) % X_SIZE, (x + 1) % X_SIZE, (x + 2) % X_SIZE

    def column(i):
        return chan, y_lo * COLUMN + i

    def at_y(step):
        other = (y + step) % Y_SIZE
        return (other // 2) * X_SIZE + x, (other % 2) * COLUMN + spot

    to_right, to_left, to_up, to_down = (y_hi * X_SIZE + right, win), (y_hi * X_SIZE + left, win), at_y(1), at_y(3)

    def other_spot(d):
        return (spot + d) % COLUMN

    order = [d for k in range(1, COLUMN // 2) for d in (k, COLUMN - k)] + [COLUMN // 2]
    peers = [column(other_spot(d)) for d in order] + [to_up, to_down, to_right, to_left]
    barrier = pltpu.get_barrier_semaphore()
    for peer in peers:
        pl.semaphore_signal(barrier, inc=1, device_id=peer, device_id_type=MESH)
    pl.semaphore_wait(barrier, len(peers))

    def remote(src, dst, send, recv, peer):
        return pltpu.make_async_remote_copy(
            src_ref=src, dst_ref=dst, send_sem=send, recv_sem=recv, device_id=peer, device_id_type=MESH)

    started = []

    def start(k, g, src, dst, recv, peer):
        copy = remote(src, dst, send_sem.at[k, g], recv, peer)
        copy.start()
        started.append(copy)

    def whole(ref, sem):
        pltpu.make_async_copy(ref, ref, sem).wait()

    spans = [pl.ds(first, count) for _, first, count in GROUPS]
    for g, bins in enumerate(spans):
        mine, theirs = r_ref.at[y_hi, x, bins, win], t_ref.at[x, bins, spot]
        pltpu.make_async_copy(s_ref.at[(1 - y_lo) * COLUMN + spot, bins], theirs, z_recv.at[0, g]).start()
        pltpu.make_async_copy(s_ref.at[win, bins], mine, z_recv.at[1, g]).start()

        def spread(d):
            i = other_spot(d)
            remote(s_ref.at[(1 - y_lo) * COLUMN + i, bins], theirs, z_send, z_recv.at[0, g], column(i)).start()
            remote(s_ref.at[y_lo * COLUMN + i, bins], mine, z_send, z_recv.at[1, g], column(i)).start()

        def both_ways(k, carry):
            spread(k)
            spread(COLUMN - k)
            return carry

        lax.fori_loop(1, COLUMN // 2, both_ways, 0)
        spread(COLUMN // 2)

    def part(chan_y, xs, bins, lo, first=0, count=COLUMN):
        return r_ref.at[chan_y, xs, bins, pl.ds(lo * COLUMN + first, count)]

    def along_y(g, bins, xs):
        mine = part(y_hi, xs, bins, y_lo)
        start(0, g, t_ref.at[xs, bins], mine, y_recv.at[0, g], to_up)
        start(1, g, t_ref.at[xs, bins], mine, y_recv.at[1, g], to_down)

    def along_y_far(g, bins, xs):
        for way, peer in ((0, to_up), (1, to_down)):
            start(2 + way, g, part(y_hi, xs, bins, y_lo, 8 * way, 8), u_ref.at[way, xs, bins], u_recv.at[way, g], peer)

    def relay_y(g, bins, xs):
        for way, peer, step in ((0, to_up, 3), (1, to_down, 1)):
            whole(u_ref.at[way, xs, bins], u_recv.at[way, g])
            other = (y + step) % Y_SIZE
            start(4 + way, g, u_ref.at[way, xs, bins], part(other // 2, xs, bins, other % 2, 8 * way, 8),
                  y_recv.at[2 + way, g], peer)

    def wait_y(g, bins, xs):
        for k, step in ((0, 3), (1, 1)):
            other = (y + step) % Y_SIZE
            whole(part(other // 2, xs, bins, other % 2), y_recv.at[k, g])
        for way in range(2):
            whole(part(1 - y_hi, xs, bins, y_lo, 8 * way, 8), y_recv.at[2 + way, g])

    def act(what, g):
        bins = spans[g]
        if what == "zy":
            whole(t_ref.at[x, bins], z_recv.at[0, g])
            along_y(g, bins, x)
            whole(part(y_hi, x, bins, y_lo), z_recv.at[1, g])
            along_y_far(g, bins, x)
        elif what == "uy":
            relay_y(g, bins, x)
        elif what == "yx":
            wait_y(g, bins, x)
            block = r_ref.at[:, x, bins]
            start(6, g, block, block, x_recv.at[0, g], to_right)
            start(7, g, block, block, x_recv.at[1, g], to_left)
        elif what == "x2y":
            whole(r_ref.at[:, left, bins], x_recv.at[0, g])
            block = r_ref.at[0, left, bins]
            start(8, g, block, block, x_recv.at[4, g], to_right)
            whole(r_ref.at[:, right, bins], x_recv.at[1, g])
            block = r_ref.at[1, right, bins]
            start(9, g, block, block, x_recv.at[5, g], to_left)
        elif what == "ey":
            for k in range(2):
                whole(r_ref.at[k, far, bins], x_recv.at[4 + k, g])
        elif what == "zx":
            block = t_ref.at[x, bins]
            whole(block, z_recv.at[0, g])
            start(6, g, block, block, x_recv.at[0, g], to_right)
            start(7, g, block, block, x_recv.at[1, g], to_left)
            block = part(y_hi, x, bins, y_lo)
            whole(block, z_recv.at[1, g])
            start(8, g, block, block, x_recv.at[2, g], to_right)
            start(9, g, block, block, x_recv.at[3, g], to_left)
        elif what == "x2x":
            block = t_ref.at[left, bins]
            whole(block, x_recv.at[0, g])
            start(10, g, block, block, x_recv.at[4, g], to_right)
            block = part(y_hi, right, bins, y_lo)
            whole(block, x_recv.at[3, g])
            start(11, g, block, block, x_recv.at[5, g], to_left)
        elif what == "y1":
            whole(t_ref.at[right, bins], x_recv.at[1, g])
            whole(part(y_hi, left, bins, y_lo), x_recv.at[2, g])
            whole(t_ref.at[far, bins], x_recv.at[4, g])
            whole(part(y_hi, far, bins, y_lo), x_recv.at[5, g])
            along_y_far(g, bins, slice(None))
            along_y(g, bins, slice(None))
        elif what == "ux":
            relay_y(g, bins, slice(None))
        elif what == "ex":
            wait_y(g, bins, slice(None))

    for what, g in ORDER:
        act(what, g)
    whole(s_ref.at[pl.ds(0, WIN - 2)], z_send)
    for copy in started:
        copy.wait_send()


def gathered_spectra(s):
    n = len(GROUPS)
    return pl.pallas_call(
        gather_kernel,
        out_shape=jax.ShapeDtypeStruct((2, X_SIZE, BINS, WIN, 8, LANES), jnp.bfloat16),
        in_specs=[pl.BlockSpec(memory_space=pltpu.VMEM)],
        out_specs=pl.BlockSpec(memory_space=pl.ANY),
        scratch_shapes=[
            pltpu.VMEM((X_SIZE, BINS, COLUMN, 8, LANES), jnp.bfloat16),
            pltpu.VMEM((2, X_SIZE, BINS, 8, 8, LANES), jnp.bfloat16),
            pltpu.SemaphoreType.DMA,
            pltpu.SemaphoreType.DMA((12, n)),
            pltpu.SemaphoreType.DMA((2, n)),
            pltpu.SemaphoreType.DMA((4, n)),
            pltpu.SemaphoreType.DMA((2, n)),
            pltpu.SemaphoreType.DMA((6, n)),
        ],
        compiler_params=pltpu.CompilerParams(
            collective_id=0, has_side_effects=True, vmem_limit_bytes=48 << 20),
        name="gather",
    )(s)


def stack_kernel(r_hbm, out_hbm, r_ref, out_ref, r_sem, out_sem):
    reads = [pltpu.make_async_copy(r_hbm.at[:, f], r_ref.at[f], r_sem.at[f]) for f in range(BINS)]
    for read in reads:
        read.start()
    chan = lax.axis_index("chan")
    row = lax.broadcasted_iota(jnp.int32, (WIN, 8, LANES), 1)
    scale = 1.0 / math.sqrt(WINDOWS)

    def one_bin(f, carry):
        pltpu.make_async_copy(r_hbm.at[:, f], r_ref.at[f], r_sem.at[f]).wait()
        own = r_ref[f, chan].astype(jnp.float32)
        turned = pltpu.roll(own.reshape(WIN, 8, LANES), 4, 1)
        turned = jnp.where(row < 4, turned, -turned).reshape(WIN * 8, LANES)
        ours = jnp.concatenate([own.T, turned.T], 0).astype(jnp.bfloat16)
        for k in range(0, CHAN, 2):
            pair = jnp.concatenate([r_ref[f, k], r_ref[f, k + 1]], 1)
            both = jnp.dot(ours, pair, preferred_element_type=jnp.float32) * scale
            lanes = slice(k * LANES, (k + 2) * LANES)
            out_ref[f, 0, :, lanes] = both[:LANES].astype(jnp.bfloat16)
            out_ref[f, 1, :, lanes] = both[LANES:].astype(jnp.bfloat16)
        pltpu.make_async_copy(out_ref.at[f], out_hbm.at[f], out_sem.at[f]).start()
        return carry

    lax.fori_loop(0, BINS, one_bin, 0)
    for f in range(BINS):
        pltpu.make_async_copy(out_ref.at[f], out_hbm.at[f], out_sem.at[f]).wait()


def stacked(r):
    anywhere = pl.BlockSpec(memory_space=pl.ANY)
    return pl.pallas_call(
        stack_kernel,
        out_shape=jax.ShapeDtypeStruct((BINS, 2, LANES, C), jnp.bfloat16),
        in_specs=[anywhere],
        out_specs=anywhere,
        scratch_shapes=[
            pltpu.VMEM((BINS, CHAN, WIN * 8, LANES), jnp.bfloat16),
            pltpu.VMEM((BINS, 2, LANES, C), jnp.bfloat16),
            pltpu.SemaphoreType.DMA((BINS,)),
            pltpu.SemaphoreType.DMA((BINS,)),
        ],
        compiler_params=pltpu.CompilerParams(vmem_limit_bytes=67043328),
        name="stack",
    )(r)


def local(raw, offsets, quality):
    s = whitened_spectra(raw, offsets, quality)
    r = gathered_spectra(s.reshape(WIN, BINS, 8, LANES))
    return stacked(r.reshape(CHAN, BINS, WIN * 8, LANES))


def solution(mesh):
    in_specs = (P("win", None, "chan"), P("win"), P("win", "chan"))
    out_specs = P("win", None, "chan", None)
    return jax.shard_map(local, mesh=mesh, in_specs=in_specs, out_specs=out_specs, check_vma=False)
```

time: 103 us -> 80.4 us (0.78)
  Pallas kernels: 94.7 us -> 78.6 us
  local copies, waits for them, and re-layouts: 7.84 us -> 1.13 us
    pallas_call x1, Pallas kernels: 74.7 us -> 62.1 us  [gathered_spectra(): pl.pallas_call(gather_kernel, out_shape=jax.ShapeDtypeStruct((2, X_SIZE,...]
    unnamed x16 -> x2, local copies, waits for them, and re-layouts: 7.84 us -> 1.13 us
    pallas_call x1, Pallas kernels: 10.9 us -> 6.22 us  [stacked(): pl.pallas_call(stack_kernel, out_shape=jax.ShapeDtypeStruct((BINS, 2, LAN...]
    pallas_call x1, Pallas kernels: 9.13 us -> 10.3 us  [whitened_spectra(): pl.pallas_call(spectra_kernel, out_shape=jax.ShapeDtypeStruct((F * 8, LAN...]
where the time goes in v3:
time: 80.4 us; the launch traced here: 79.8 us
  Pallas kernels  78.6 us (98%)
  local copies, waits for them, and re-layouts  1.13 us (1%)
    pallas_call x1, Pallas kernels, gathered_spectra(): pl.pallas_call(gather_kernel, out_shape=jax.ShapeDtypeStruct((2, X_SIZE,...  62.1 us
    pallas_call x1, Pallas kernels, whitened_spectra(): pl.pallas_call(spectra_kernel, out_shape=jax.ShapeDtypeStruct((F * 8, LAN...  10.3 us
    pallas_call x1, Pallas kernels, stacked(): pl.pallas_call(stack_kernel, out_shape=jax.ShapeDtypeStruct((BINS, 2, LAN...  6.22 us

profile of v3, /device:TPU:32, one launch (start us, length us, event | category | flops | bytes accessed | tf_op | source)
XLA Modules:
  0.0 79.8 jit_solution(14403098415198134135)
XLA Ops:
  0.0 10.3 %spectra.1 = bf16[3072,128]{1,0:T(8,128)(2,1)} custom-call(s32[4]{0:T(128)} %off_hbm.1, s32[4,128]{1,0:T(4,128)} %quality_hbm.1, f32[4,384,128]{2,1,0:T(8,128)} %constant.2.clone.seeds_hbm, bf16[4,3200,128]{2,1,0:T(8,128)(2,1)} %raw_hbm.1), custom_call_target="tpu_custom_call" | custom-call | tf_op jit(solution)/shard_map/spectra/pallas_call | solution.py:94
  10.3 0.0 copy-start
  10.3 1.1 %copy-done = bf16[3072,128]{1,0:T(8,128)(2,1)S(1)} copy-done((bf16[3072,128]{1,0:T(8,128)(2,1)S(1)}, bf16[3072,128]{1,0:T(8,128)(2,1)}, u32[]{:S(2)}) %copy-start) | copy-done | bytes 786456
  11.4 62.1 %gather.1 = bf16[2,4,12,32,8,128]{5,4,3,2,1,0:T(8,128)(2,1)} custom-call(bf16[32,12,8,128]{3,2,1,0:T(8,128)(2,1)S(1)} %bitcast.2), custom_call_target="tpu_custom_call" | custom-call | tf_op jit(solution)/shard_map/gather/pallas_call | solution.py:262
  73.5 6.2 %stack.1 = bf16[12,2,128,1024]{3,2,1,0:T(8,128)(2,1)} custom-call(bf16[8,12,256,128]{3,2,1,0:T(8,128)(2,1)} %bitcast.3), custom_call_target="tpu_custom_call" | custom-call | tf_op jit(solution)/shard_map/stack/pallas_call | solution.py:313
Async XLA Ops:
  10.3 1.1 %copy-start = (bf16[3072,128]{1,0:T(8,128)(2,1)S(1)}, bf16[3072,128]{1,0:T(8,128)(2,1)}, u32[]{:S(2)}) copy-start(bf16[3072,128]{1,0:T(8,128)(2,1)} %spectra.1) | copy-start | bytes 2359300

commit v4 on v3

--- a/solution.py
+++ b/solution.py
@@ -24,12 +24,12 @@
 CHAN, WIN = 8, 32
 GROUPS = (("y", 0, 1), ("x", 1, 1), ("y", 2, 2), ("x", 4, 2), ("x", 6, 2), ("y", 8, 2), ("y", 10, 1), ("y", 11, 1))
 ORDER = (
-    ("zy", 0), ("zx", 1), ("uy", 0), ("zy", 2), ("x2x", 1), ("yx", 0),
-    ("y1", 1), ("zx", 3), ("uy", 2), ("x2y", 0), ("ux", 1), ("zx", 4),
+    ("zy", 0), ("zx", 1), ("zy", 2), ("x2x", 1), ("yx", 0),
+    ("y1", 1), ("zx", 3), ("x2y", 0), ("zx", 4),
     ("x2x", 3), ("zy", 5), ("yx", 2), ("ey", 0), ("zy", 6), ("ex", 1),
-    ("zy", 7), ("x2x", 4), ("uy", 5), ("y1", 3), ("uy", 6), ("uy", 7),
-    ("yx", 5), ("ux", 3), ("x2y", 2), ("y1", 4), ("yx", 6), ("yx", 7),
-    ("x2y", 5), ("ex", 3), ("ey", 2), ("ux", 4), ("x2y", 6), ("x2y", 7),
+    ("zy", 7), ("x2x", 4), ("y1", 3),
+    ("yx", 5), ("x2y", 2), ("y1", 4), ("yx", 6), ("yx", 7),
+    ("x2y", 5), ("ex", 3), ("ey", 2), ("x2y", 6), ("x2y", 7),
     ("ey", 5), ("ex", 4), ("ey", 6), ("ey", 7),
 )
 MESH = pl.DeviceIdType.MESH
@@ -43,27 +43,32 @@
     return np.stack([np.cos(first), -np.sin(first), np.cos(turn), -np.sin(turn)]).astype(np.float32)
 
 
-def spectra_kernel(off_hbm, quality_hbm, seeds_hbm, raw_hbm, out_ref,
-                   off_ref, quality_ref, seeds, table, rows, wide, pair, product, mixed, sem):
+def spectra_kernel(off_hbm, quality_hbm, seeds_hbm, raw_hbm, s_ref,
+                   off_ref, quality_ref, seeds, table, rows, wide, pairs, product, mixed, sem):
     seeds_copy = pltpu.make_async_copy(seeds_hbm, seeds, sem.at[LOCAL_W])
     small = [pltpu.make_async_copy(off_hbm, off_ref, sem.at[LOCAL_W + 1]),
              pltpu.make_async_copy(quality_hbm, quality_ref, sem.at[LOCAL_W + 2])]
     copies = [pltpu.make_async_copy(raw_hbm.at[w], rows.at[w], sem.at[w]) for w in range(LOCAL_W)]
-    for copy in [seeds_copy] + small + copies:
+    for copy in [seeds_copy] + small + copies[:1]:
         copy.start()
     seeds_copy.wait()
-
-    step = 48
+    for copy in copies[1:]:
+        copy.start()
+
+    step, half_blocks = 48, L // LANES // 2
+    row = lax.broadcasted_iota(jnp.int32, (step, LANES), 0)
+    sign = jnp.where(row % 2 == FIRST_BIN % 2, 1.0, -1.0).astype(jnp.bfloat16)
 
     def table_rows(i, carry):
         at = pl.multiple_of(i * step, 16)
-        here = pl.ds(at, step)
-        below = pl.ds(pl.multiple_of(F + at, 16), step)
-        c, m = seeds[0, here, :], seeds[1, here, :]
-        tc, tm = seeds[2, here, :], seeds[3, here, :]
-        for a in range(L // LANES):
-            table[here, a * LANES:(a + 1) * LANES] = c.astype(jnp.bfloat16)
-            table[below, a * LANES:(a + 1) * LANES] = m.astype(jnp.bfloat16)
+        c, m = seeds[0, pl.ds(at, step), :], seeds[1, pl.ds(at, step), :]
+        tc, tm = seeds[2, pl.ds(at, step), :], seeds[3, pl.ds(at, step), :]
+        for a in range(half_blocks):
+            for v, first in ((c, at), (m, pl.multiple_of(F + at, 16))):
+                v = v.astype(jnp.bfloat16)
+                here = pl.ds(first, step)
+                table[here, a * LANES:(a + 1) * LANES] = v
+                table[here, (a + half_blocks) * LANES:(a + half_blocks + 1) * LANES] = v * sign
             c, m = c * tc - m * tm, m * tc + c * tm
         return carry
 
@@ -71,13 +76,22 @@
     for copy in small:
         copy.wait()
 
+    def cut(w, lo, hi):
+        if lo == 0:
+            copies[w].wait()
+            wide[w % 2] = rows[w].astype(jnp.float32)
+        lanes = slice(w % 2 * LANES, (w % 2 + 1) * LANES)
+        pairs[w // 2, lo:hi, lanes] = wide[w % 2, pl.ds(off_ref[w] + lo, hi - lo), :].astype(jnp.bfloat16)
+
+    cut(0, 0, L)
+    cut(1, 0, L)
     for first in range(0, LOCAL_W, 2):
-        for half in range(2):
-            w = first + half
-            copies[w].wait()
-            wide[half] = rows[w].astype(jnp.float32)
-            pair[:, half * LANES:(half + 1) * LANES] = wide[half, pl.ds(off_ref[w], L), :].astype(jnp.bfloat16)
-        product[...] = jnp.dot(table[...], pair[...], preferred_element_type=jnp.float32)
+        chunk, tile = L // 3, 2 * F // 6
+        for i in range(6):
+            at = slice(i * tile, (i + 1) * tile)
+            product[at] = jnp.dot(table[at], pairs[first // 2], preferred_element_type=jnp.float32)
+            if first + 2 < LOCAL_W:
+                cut(first + 2 + i // 3, i % 3 * chunk, (i % 3 + 1) * chunk)
         power = jnp.sum(product[...] * product[...], axis=0, keepdims=True) / F
         whiten = lax.rsqrt(power + EPSILON)
         for half in range(2):
@@ -86,34 +100,14 @@
             gain = whiten[:, lanes] * quality_ref[w:w + 1, :].astype(jnp.float32)
             for p in range(2):
                 mixed[pl.ds(p * LOCAL_W + w, F, stride=8), :] = product[p * F:(p + 1) * F, lanes] * gain
-    out_ref[...] = mixed[...].astype(jnp.bfloat16)
-
-
-def whitened_spectra(raw, offsets, quality):
-    anywhere = pl.BlockSpec(memory_space=pl.ANY)
-    return pl.pallas_call(
-        spectra_kernel,
-        out_shape=jax.ShapeDtypeStruct((F * 8, LANES), jnp.bfloat16),
-        in_specs=[anywhere] * 4,
-        out_specs=pl.BlockSpec(memory_space=pltpu.VMEM),
-        scratch_shapes=[
-            pltpu.SMEM((LOCAL_W,), jnp.int32),
-            pltpu.VMEM((LOCAL_W, LANES), jnp.int32),
-            pltpu.VMEM((4, F, LANES), jnp.float32),
-            pltpu.VMEM((2 * F, L), jnp.bfloat16),
-            pltpu.VMEM((LOCAL_W, SEG, LANES), jnp.bfloat16),
-            pltpu.VMEM((2, SEG, LANES), jnp.float32),
-            pltpu.VMEM((L, 2 * LANES), jnp.bfloat16),
-            pltpu.VMEM((2 * F, 2 * LANES), jnp.float32),
-            pltpu.VMEM((F * 8, LANES), jnp.float32),
-            pltpu.SemaphoreType.DMA((LOCAL_W + 3,)),
-        ],
-        compiler_params=pltpu.CompilerParams(vmem_limit_bytes=67043328),
-        name="spectra",
-    )(offsets, quality, jnp.asarray(table_seeds()), raw)
-
-
-def gather_kernel(s_ref, r_ref, t_ref, u_ref, z_send, send_sem, z_recv, y_recv, u_recv, x_recv):
+    s_ref[...] = mixed[...].astype(jnp.bfloat16).reshape(WIN, BINS, 8, LANES)
+
+
+def gather_kernel(off_hbm, quality_hbm, seeds_hbm, raw_hbm, r_ref,
+                  s_ref, t_ref, z_send, send_sem, z_recv, y_recv, x_recv, *spectra_scratch):
+    def spectra():
+        spectra_kernel(off_hbm, quality_hbm, seeds_hbm, raw_hbm, s_ref, *spectra_scratch)
+
     chan, win = lax.axis_index("chan"), lax.axis_index("win")
     y_hi, x = chan // X_SIZE, chan % X_SIZE
     y_lo, spot = win // COLUMN, win % COLUMN
@@ -133,10 +127,12 @@
         return (spot + d) % COLUMN
 
     order = [d for k in range(1, COLUMN // 2) for d in (k, COLUMN - k)] + [COLUMN // 2]
-    peers = [column(other_spot(d)) for d in order] + [to_up, to_down, to_right, to_left]
+    peers = [column(other_spot(d)) for d in order] + [to_up, to_down, at_y(2), to_right, to_left]
     barrier = pltpu.get_barrier_semaphore()
     for peer in peers:
         pl.semaphore_signal(barrier, inc=1, device_id=peer, device_id_type=MESH)
+
+    spectra()
     pl.semaphore_wait(barrier, len(peers))
 
     def remote(src, dst, send, recv, peer):
@@ -181,22 +177,14 @@
         start(1, g, t_ref.at[xs, bins], mine, y_recv.at[1, g], to_down)
 
     def along_y_far(g, bins, xs):
-        for way, peer in ((0, to_up), (1, to_down)):
-            start(2 + way, g, part(y_hi, xs, bins, y_lo, 8 * way, 8), u_ref.at[way, xs, bins], u_recv.at[way, g], peer)
-
-    def relay_y(g, bins, xs):
-        for way, peer, step in ((0, to_up, 3), (1, to_down, 1)):
-            whole(u_ref.at[way, xs, bins], u_recv.at[way, g])
-            other = (y + step) % Y_SIZE
-            start(4 + way, g, u_ref.at[way, xs, bins], part(other // 2, xs, bins, other % 2, 8 * way, 8),
-                  y_recv.at[2 + way, g], peer)
+        block = part(y_hi, xs, bins, y_lo)
+        start(2, g, block, block, y_recv.at[2, g], at_y(2))
 
     def wait_y(g, bins, xs):
         for k, step in ((0, 3), (1, 1)):
             other = (y + step) % Y_SIZE
             whole(part(other // 2, xs, bins, other % 2), y_recv.at[k, g])
-        for way in range(2):
-            whole(part(1 - y_hi, xs, bins, y_lo, 8 * way, 8), y_recv.at[2 + way, g])
+        whole(part(1 - y_hi, xs, bins, y_lo), y_recv.at[2, g])
 
     def act(what, g):
         bins = spans[g]
@@ -205,8 +193,6 @@
             along_y(g, bins, x)
             whole(part(y_hi, x, bins, y_lo), z_recv.at[1, g])
             along_y_far(g, bins, x)
-        elif what == "uy":
-            relay_y(g, bins, x)
         elif what == "yx":
             wait_y(g, bins, x)
             block = r_ref.at[:, x, bins]
@@ -245,8 +231,6 @@
             whole(part(y_hi, far, bins, y_lo), x_recv.at[5, g])
             along_y_far(g, bins, slice(None))
             along_y(g, bins, slice(None))
-        elif what == "ux":
-            relay_y(g, bins, slice(None))
         elif what == "ex":
             wait_y(g, bins, slice(None))
 
@@ -257,45 +241,51 @@
         copy.wait_send()
 
 
-def gathered_spectra(s):
+def gathered_spectra(raw, offsets, quality):
     n = len(GROUPS)
+    inputs = [pltpu.with_memory_space_constraint(a, pltpu.HBM) for a in (offsets, quality, jnp.asarray(table_seeds()), raw)]
     return pl.pallas_call(
         gather_kernel,
         out_shape=jax.ShapeDtypeStruct((2, X_SIZE, BINS, WIN, 8, LANES), jnp.bfloat16),
-        in_specs=[pl.BlockSpec(memory_space=pltpu.VMEM)],
-        out_specs=pl.BlockSpec(memory_space=pl.ANY),
+        in_specs=[pl.BlockSpec(memory_space=pltpu.HBM)] * 4,
+        out_specs=pl.BlockSpec(memory_space=pltpu.VMEM),
         scratch_shapes=[
+            pltpu.VMEM((WIN, BINS, 8, LANES), jnp.bfloat16),
             pltpu.VMEM((X_SIZE, BINS, COLUMN, 8, LANES), jnp.bfloat16),
-            pltpu.VMEM((2, X_SIZE, BINS, 8, 8, LANES), jnp.bfloat16),
             pltpu.SemaphoreType.DMA,
             pltpu.SemaphoreType.DMA((12, n)),
             pltpu.SemaphoreType.DMA((2, n)),
-            pltpu.SemaphoreType.DMA((4, n)),
-            pltpu.SemaphoreType.DMA((2, n)),
+            pltpu.SemaphoreType.DMA((3, n)),
             pltpu.SemaphoreType.DMA((6, n)),
+            pltpu.SMEM((LOCAL_W,), jnp.int32),
+            pltpu.VMEM((LOCAL_W, LANES), jnp.int32),
+            pltpu.VMEM((4, F, LANES), jnp.float32),
+            pltpu.VMEM((2 * F, L), jnp.bfloat16),
+            pltpu.VMEM((LOCAL_W, SEG, LANES), jnp.bfloat16),
+            pltpu.VMEM((2, SEG, LANES), jnp.float32),
+            pltpu.VMEM((2, L, 2 * LANES), jnp.bfloat16),
+            pltpu.VMEM((2 * F, 2 * LANES), jnp.float32),
+            pltpu.VMEM((F * 8, LANES), jnp.float32),
+            pltpu.SemaphoreType.DMA((LOCAL_W + 3,)),
         ],
         compiler_params=pltpu.CompilerParams(
-            collective_id=0, has_side_effects=True, vmem_limit_bytes=48 << 20),
+            collective_id=0, has_side_effects=True, vmem_limit_bytes=40 << 20),
         name="gather",
-    )(s)
-
-
-def stack_kernel(r_hbm, out_hbm, r_ref, out_ref, r_sem, out_sem):
-    reads = [pltpu.make_async_copy(r_hbm.at[:, f], r_ref.at[f], r_sem.at[f]) for f in range(BINS)]
-    for read in reads:
-        read.start()
+    )(*inputs)
+
+
+def stack_kernel(r_ref, out_hbm, out_ref, out_sem):
     chan = lax.axis_index("chan")
     row = lax.broadcasted_iota(jnp.int32, (WIN, 8, LANES), 1)
     scale = 1.0 / math.sqrt(WINDOWS)
 
     def one_bin(f, carry):
-        pltpu.make_async_copy(r_hbm.at[:, f], r_ref.at[f], r_sem.at[f]).wait()
-        own = r_ref[f, chan].astype(jnp.float32)
+        own = r_ref[chan, f].astype(jnp.float32)
         turned = pltpu.roll(own.reshape(WIN, 8, LANES), 4, 1)
         turned = jnp.where(row < 4, turned, -turned).reshape(WIN * 8, LANES)
         ours = jnp.concatenate([own.T, turned.T], 0).astype(jnp.bfloat16)
         for k in range(0, CHAN, 2):
-            pair = jnp.concatenate([r_ref[f, k], r_ref[f, k + 1]], 1)
+            pair = jnp.concatenate([r_ref[k, f], r_ref[k + 1, f]], 1)
             both = jnp.dot(ours, pair, preferred_element_type=jnp.float32) * scale
             lanes = slice(k * LANES, (k + 2) * LANES)
             out_ref[f, 0, :, lanes] = both[:LANES].astype(jnp.bfloat16)
@@ -309,26 +299,22 @@
 
 
 def stacked(r):
-    anywhere = pl.BlockSpec(memory_space=pl.ANY)
     return pl.pallas_call(
         stack_kernel,
         out_shape=jax.ShapeDtypeStruct((BINS, 2, LANES, C), jnp.bfloat16),
-        in_specs=[anywhere],
-        out_specs=anywhere,
+        in_specs=[pl.BlockSpec(memory_space=pltpu.VMEM)],
+        out_specs=pl.BlockSpec(memory_space=pl.ANY),
         scratch_shapes=[
-            pltpu.VMEM((BINS, CHAN, WIN * 8, LANES), jnp.bfloat16),
             pltpu.VMEM((BINS, 2, LANES, C), jnp.bfloat16),
             pltpu.SemaphoreType.DMA((BINS,)),
-            pltpu.SemaphoreType.DMA((BINS,)),
         ],
-        compiler_params=pltpu.CompilerParams(vmem_limit_bytes=67043328),
+        compiler_params=pltpu.CompilerParams(vmem_limit_bytes=24 << 20),
         name="stack",
     )(r)
 
 
 def local(raw, offsets, quality):
-    s = whitened_spectra(raw, offsets, quality)
-    r = gathered_spectra(s.reshape(WIN, BINS, 8, LANES))
+    r = gathered_spectra(raw, offsets, quality)
     return stacked(r.reshape(CHAN, BINS, WIN * 8, LANES))
 
 

time: 80.4 us -> 70.5 us (0.88)
  Pallas kernels: 78.6 us -> 69.6 us
  local copies, waits for them, and re-layouts: 1.13 us -> 0 us
    pallas_call x1 -> x0, Pallas kernels: 10.3 us -> none  [whitened_spectra(): pl.pallas_call(spectra_kernel, out_shape=jax.ShapeDtypeStruct((F * 8, LAN...]
    pallas_call x1, Pallas kernels: 62.1 us -> 64.5 us  [gathered_spectra(): pl.pallas_call(gather_kernel, out_shape=jax.ShapeDtypeStruct((2, X_SIZE,...]
    pallas_call x1, Pallas kernels: 6.22 us -> 5.07 us  [stacked(): pl.pallas_call(stack_kernel, out_shape=jax.ShapeDtypeStruct((BINS, 2, LAN...]
    unnamed x2 -> x0, local copies, waits for them, and re-layouts: 1.13 us -> none
where the time goes in v4:
time: 70.5 us; the launch traced here: 69.6 us
  Pallas kernels  69.6 us (99%)
    pallas_call x1, Pallas kernels, gathered_spectra(): pl.pallas_call(gather_kernel, out_shape=jax.ShapeDtypeStruct((2, X_SIZE,...  64.5 us
    pallas_call x1, Pallas kernels, stacked(): pl.pallas_call(stack_kernel, out_shape=jax.ShapeDtypeStruct((BINS, 2, LAN...  5.07 us

profile of v4, /device:TPU:32, one launch (start us, length us, event | category | flops | bytes accessed | tf_op | source)
XLA Modules:
  0.0 69.6 jit_solution(8078776713037555013)
XLA Ops:
  0.0 64.5 %gather.1 = bf16[2,4,12,32,8,128]{5,4,3,2,1,0:T(8,128)(2,1)S(1)} custom-call(s32[4]{0:T(128)} %off_hbm.1, s32[4,128]{1,0:T(4,128)} %quality_hbm.1, f32[4,384,128]{2,1,0:T(8,128)} %constant.2.clone.seeds_hbm, bf16[4,3200,128]{2,1,0:T(8,128)(2,1)} %raw_hbm.1), custom_call_target="tpu_custom_call" | custom-call | tf_op jit(solution)/shard_map/gather/pallas_call | solution.py:247
  64.5 5.1 %stack.1 = bf16[12,2,128,1024]{3,2,1,0:T(8,128)(2,1)} custom-call(bf16[8,12,256,128]{3,2,1,0:T(8,128)(2,1)S(1)} %bitcast.1), custom_call_target="tpu_custom_call" | custom-call | tf_op jit(solution)/shard_map/stack/pallas_call | solution.py:302

commit v5 on v4

--- a/solution.py
+++ b/solution.py
@@ -22,15 +22,14 @@
 X_SIZE, Y_SIZE, Z_SIZE = 4, 4, 8
 COLUMN = 2 * Z_SIZE
 CHAN, WIN = 8, 32
-GROUPS = (("y", 0, 1), ("x", 1, 1), ("y", 2, 2), ("x", 4, 2), ("x", 6, 2), ("y", 8, 2), ("y", 10, 1), ("y", 11, 1))
+GROUPS = (('p', 0, 1), ('p', 1, 1), ('p', 2, 1), ('y', 3, 1), ('x', 4, 1), ('y', 5, 1), ('y', 6, 1), ('y', 7, 2), ('y', 9, 3))
 ORDER = (
-    ("zy", 0), ("zx", 1), ("zy", 2), ("x2x", 1), ("yx", 0),
-    ("y1", 1), ("zx", 3), ("x2y", 0), ("zx", 4),
-    ("x2x", 3), ("zy", 5), ("yx", 2), ("ey", 0), ("zy", 6), ("ex", 1),
-    ("zy", 7), ("x2x", 4), ("y1", 3),
-    ("yx", 5), ("x2y", 2), ("y1", 4), ("yx", 6), ("yx", 7),
-    ("x2y", 5), ("ex", 3), ("ey", 2), ("x2y", 6), ("x2y", 7),
-    ("ey", 5), ("ex", 4), ("ey", 6), ("ey", 7),
+    ("x2p", 0), ("zy", 3), ("x2p", 1), ("zx", 4), ("zy", 5), ("x2p", 2),
+    ("yx", 3), ("x2x", 4), ("zp", 0), ("zy", 6), ("zp", 1), ("zp", 2),
+    ("zy", 7), ("yx", 5), ("yx", 6), ("y1", 4), ("x2y", 3), ("x2y", 5),
+    ("yx", 7), ("zy", 8), ("y1", 0), ("x2y", 6), ("yx", 8), ("x2y", 7),
+    ("ex", 4), ("ey", 5), ("y1", 1), ("y1", 2), ("x2y", 8), ("ey", 7),
+    ("ey", 3), ("ex", 0), ("ex", 2), ("ey", 6), ("ex", 1), ("ey", 8),
 )
 MESH = pl.DeviceIdType.MESH
 
@@ -100,11 +99,11 @@
             gain = whiten[:, lanes] * quality_ref[w:w + 1, :].astype(jnp.float32)
             for p in range(2):
                 mixed[pl.ds(p * LOCAL_W + w, F, stride=8), :] = product[p * F:(p + 1) * F, lanes] * gain
-    s_ref[...] = mixed[...].astype(jnp.bfloat16).reshape(WIN, BINS, 8, LANES)
+    s_ref[...] = mixed[...].astype(jnp.bfloat16).reshape(2, COLUMN, BINS, 8, LANES)
 
 
 def gather_kernel(off_hbm, quality_hbm, seeds_hbm, raw_hbm, r_ref,
-                  s_ref, t_ref, z_send, send_sem, z_recv, y_recv, x_recv, *spectra_scratch):
+                  s_ref, t_ref, p_ref, z_send, send_sem, z_recv, y_recv, x_recv, p_sem, own_sem, *spectra_scratch):
     def spectra():
         spectra_kernel(off_hbm, quality_hbm, seeds_hbm, raw_hbm, s_ref, *spectra_scratch)
 
@@ -150,15 +149,13 @@
         pltpu.make_async_copy(ref, ref, sem).wait()
 
     spans = [pl.ds(first, count) for _, first, count in GROUPS]
-    for g, bins in enumerate(spans):
-        mine, theirs = r_ref.at[y_hi, x, bins, win], t_ref.at[x, bins, spot]
-        pltpu.make_async_copy(s_ref.at[(1 - y_lo) * COLUMN + spot, bins], theirs, z_recv.at[0, g]).start()
-        pltpu.make_async_copy(s_ref.at[win, bins], mine, z_recv.at[1, g]).start()
+
+    def along_z(source, landing, send, g):
+        pltpu.make_async_copy(source(spot), landing, z_recv.at[g]).start()
 
         def spread(d):
             i = other_spot(d)
-            remote(s_ref.at[(1 - y_lo) * COLUMN + i, bins], theirs, z_send, z_recv.at[0, g], column(i)).start()
-            remote(s_ref.at[y_lo * COLUMN + i, bins], mine, z_send, z_recv.at[1, g], column(i)).start()
+            remote(source(i), landing, send, z_recv.at[g], column(i)).start()
 
         def both_ways(k, carry):
             spread(k)
@@ -168,31 +165,41 @@
         lax.fori_loop(1, COLUMN // 2, both_ways, 0)
         spread(COLUMN // 2)
 
-    def part(chan_y, xs, bins, lo, first=0, count=COLUMN):
-        return r_ref.at[chan_y, xs, bins, pl.ds(lo * COLUMN + first, count)]
+    every = slice(None)
+    early = 0
+    for g, bins in enumerate(spans):
+        if GROUPS[g][0] == "p":
+            early += GROUPS[g][2]
+            block = s_ref.at[:, :, bins]
+            start(6, g, block, p_ref.at[x, :, :, bins], x_recv.at[0, g], to_right)
+            start(7, g, block, p_ref.at[x, :, :, bins], x_recv.at[1, g], to_left)
+            pltpu.make_async_copy(block, p_ref.at[x, :, :, bins], p_sem.at[0, g]).start()
+    for g, bins in enumerate(spans):
+        if GROUPS[g][0] != "p":
+            along_z(lambda i: s_ref.at[:, i, bins], t_ref.at[x, :, bins, spot], z_send, g)
+
+    def part(chan_y, xs, bins, lo):
+        return r_ref.at[chan_y, xs, bins, pl.ds(lo * COLUMN, COLUMN)]
 
     def along_y(g, bins, xs):
-        mine = part(y_hi, xs, bins, y_lo)
-        start(0, g, t_ref.at[xs, bins], mine, y_recv.at[0, g], to_up)
-        start(1, g, t_ref.at[xs, bins], mine, y_recv.at[1, g], to_down)
-
-    def along_y_far(g, bins, xs):
-        block = part(y_hi, xs, bins, y_lo)
-        start(2, g, block, block, y_recv.at[2, g], at_y(2))
+        landing = part(y_hi, xs, bins, y_lo)
+        other, own = t_ref.at[xs, 1 - y_lo, bins], t_ref.at[xs, y_lo, bins]
+        start(0, g, other, landing, y_recv.at[0, g], to_up)
+        start(1, g, other, landing, y_recv.at[1, g], to_down)
+        start(2, g, own, landing, y_recv.at[2, g], at_y(2))
+        pltpu.make_async_copy(own, landing, own_sem.at[g]).start()
 
     def wait_y(g, bins, xs):
-        for k, step in ((0, 3), (1, 1)):
+        for k, step in ((0, 3), (1, 1), (2, 2)):
             other = (y + step) % Y_SIZE
             whole(part(other // 2, xs, bins, other % 2), y_recv.at[k, g])
-        whole(part(1 - y_hi, xs, bins, y_lo), y_recv.at[2, g])
+        whole(part(y_hi, xs, bins, y_lo), own_sem.at[g])
 
     def act(what, g):
         bins = spans[g]
         if what == "zy":
-            whole(t_ref.at[x, bins], z_recv.at[0, g])
+            whole(t_ref.at[x, :, bins], z_recv.at[g])
             along_y(g, bins, x)
-            whole(part(y_hi, x, bins, y_lo), z_recv.at[1, g])
-            along_y_far(g, bins, x)
         elif what == "yx":
             wait_y(g, bins, x)
             block = r_ref.at[:, x, bins]
@@ -201,42 +208,53 @@
         elif what == "x2y":
             whole(r_ref.at[:, left, bins], x_recv.at[0, g])
             block = r_ref.at[0, left, bins]
-            start(8, g, block, block, x_recv.at[4, g], to_right)
+            start(8, g, block, block, x_recv.at[2, g], to_right)
             whole(r_ref.at[:, right, bins], x_recv.at[1, g])
             block = r_ref.at[1, right, bins]
-            start(9, g, block, block, x_recv.at[5, g], to_left)
+            start(9, g, block, block, x_recv.at[3, g], to_left)
         elif what == "ey":
             for k in range(2):
-                whole(r_ref.at[k, far, bins], x_recv.at[4 + k, g])
+                whole(r_ref.at[k, far, bins], x_recv.at[2 + k, g])
         elif what == "zx":
-            block = t_ref.at[x, bins]
-            whole(block, z_recv.at[0, g])
+            block = t_ref.at[x, :, bins]
+            whole(block, z_recv.at[g])
             start(6, g, block, block, x_recv.at[0, g], to_right)
             start(7, g, block, block, x_recv.at[1, g], to_left)
-            block = part(y_hi, x, bins, y_lo)
-            whole(block, z_recv.at[1, g])
+        elif what == "x2x":
+            whole(t_ref.at[left, :, bins], x_recv.at[0, g])
+            block = t_ref.at[left, 0, bins]
             start(8, g, block, block, x_recv.at[2, g], to_right)
+            whole(t_ref.at[right, :, bins], x_recv.at[1, g])
+            block = t_ref.at[right, 1, bins]
             start(9, g, block, block, x_recv.at[3, g], to_left)
-        elif what == "x2x":
-            block = t_ref.at[left, bins]
-            whole(block, x_recv.at[0, g])
-            start(10, g, block, block, x_recv.at[4, g], to_right)
-            block = part(y_hi, right, bins, y_lo)
-            whole(block, x_recv.at[3, g])
-            start(11, g, block, block, x_recv.at[5, g], to_left)
+        elif what == "x2p":
+            whole(p_ref.at[left, :, :, bins], x_recv.at[0, g])
+            block = p_ref.at[left, 0, :, bins]
+            start(8, g, block, block, x_recv.at[2, g], to_right)
+            whole(p_ref.at[right, :, :, bins], x_recv.at[1, g])
+            block = p_ref.at[right, 1, :, bins]
+            start(9, g, block, block, x_recv.at[3, g], to_left)
+        elif what == "zp":
+            whole(p_ref.at[x, :, :, bins], p_sem.at[0, g])
+            for k in range(2):
+                whole(p_ref.at[far, k, :, bins], x_recv.at[2 + k, g])
+            along_z(lambda i: p_ref.at[:, :, i, bins], t_ref.at[:, :, bins, spot], p_sem.at[1, g], g)
         elif what == "y1":
-            whole(t_ref.at[right, bins], x_recv.at[1, g])
-            whole(part(y_hi, left, bins, y_lo), x_recv.at[2, g])
-            whole(t_ref.at[far, bins], x_recv.at[4, g])
-            whole(part(y_hi, far, bins, y_lo), x_recv.at[5, g])
-            along_y_far(g, bins, slice(None))
-            along_y(g, bins, slice(None))
+            if GROUPS[g][0] == "p":
+                whole(t_ref.at[:, :, bins], z_recv.at[g])
+            else:
+                for k in range(2):
+                    whole(t_ref.at[far, k, bins], x_recv.at[2 + k, g])
+            along_y(g, bins, every)
         elif what == "ex":
-            wait_y(g, bins, slice(None))
+            wait_y(g, bins, every)
 
     for what, g in ORDER:
         act(what, g)
-    whole(s_ref.at[pl.ds(0, WIN - 2)], z_send)
+    whole(s_ref.at[:, pl.ds(0, COLUMN - 1), pl.ds(0, BINS - early)], z_send)
+    for g, bins in enumerate(spans):
+        if GROUPS[g][0] == "p":
+            whole(p_ref.at[:, :, pl.ds(0, COLUMN - 1), bins], p_sem.at[1, g])
     for copy in started:
         copy.wait_send()
 
@@ -250,13 +268,16 @@
         in_specs=[pl.BlockSpec(memory_space=pltpu.HBM)] * 4,
         out_specs=pl.BlockSpec(memory_space=pltpu.VMEM),
         scratch_shapes=[
-            pltpu.VMEM((WIN, BINS, 8, LANES), jnp.bfloat16),
-            pltpu.VMEM((X_SIZE, BINS, COLUMN, 8, LANES), jnp.bfloat16),
+            pltpu.VMEM((2, COLUMN, BINS, 8, LANES), jnp.bfloat16),
+            pltpu.VMEM((X_SIZE, 2, BINS, COLUMN, 8, LANES), jnp.bfloat16),
+            pltpu.VMEM((X_SIZE, 2, COLUMN, BINS, 8, LANES), jnp.bfloat16),
             pltpu.SemaphoreType.DMA,
-            pltpu.SemaphoreType.DMA((12, n)),
+            pltpu.SemaphoreType.DMA((10, n)),
+            pltpu.SemaphoreType.DMA((n,)),
+            pltpu.SemaphoreType.DMA((3, n)),
+            pltpu.SemaphoreType.DMA((4, n)),
             pltpu.SemaphoreType.DMA((2, n)),
-            pltpu.SemaphoreType.DMA((3, n)),
-            pltpu.SemaphoreType.DMA((6, n)),
+            pltpu.SemaphoreType.DMA((n,)),
             pltpu.SMEM((LOCAL_W,), jnp.int32),
             pltpu.VMEM((LOCAL_W, LANES), jnp.int32),
             pltpu.VMEM((4, F, LANES), jnp.float32),

time: 70.5 us -> 67 us (0.950)
  Pallas kernels: 69.6 us -> 66.1 us
    pallas_call x1, Pallas kernels: 64.5 us -> 61 us  [gathered_spectra(): pl.pallas_call(gather_kernel, out_shape=jax.ShapeDtypeStruct((2, X_SIZE,...]
where the time goes in v5:
time: 67 us; the launch traced here: 66.1 us
  Pallas kernels  66.1 us (99%)
    pallas_call x1, Pallas kernels, gathered_spectra(): pl.pallas_call(gather_kernel, out_shape=jax.ShapeDtypeStruct((2, X_SIZE,...  61 us
    pallas_call x1, Pallas kernels, stacked(): pl.pallas_call(stack_kernel, out_shape=jax.ShapeDtypeStruct((BINS, 2, LAN...  5.07 us

profile of v5, /device:TPU:32, one launch (start us, length us, event | category | flops | bytes accessed | tf_op | source)
XLA Modules:
  0.0 66.1 jit_solution(6043572661197116721)
XLA Ops:
  0.0 61.0 %gather.1 = bf16[2,4,12,32,8,128]{5,4,3,2,1,0:T(8,128)(2,1)S(1)} custom-call(s32[4]{0:T(128)} %off_hbm.1, s32[4,128]{1,0:T(4,128)} %quality_hbm.1, f32[4,384,128]{2,1,0:T(8,128)} %constant.2.clone.seeds_hbm, bf16[4,3200,128]{2,1,0:T(8,128)(2,1)} %raw_hbm.1), custom_call_target="tpu_custom_call" | custom-call | tf_op jit(solution)/shard_map/gather/pallas_call | solution.py:265
  61.0 5.1 %stack.1 = bf16[12,2,128,1024]{3,2,1,0:T(8,128)(2,1)} custom-call(bf16[8,12,256,128]{3,2,1,0:T(8,128)(2,1)S(1)} %bitcast.1), custom_call_target="tpu_custom_call" | custom-call | tf_op jit(solution)/shard_map/stack/pallas_call | solution.py:323

commit v6 on v5

--- a/solution.py
+++ b/solution.py
@@ -22,14 +22,14 @@
 X_SIZE, Y_SIZE, Z_SIZE = 4, 4, 8
 COLUMN = 2 * Z_SIZE
 CHAN, WIN = 8, 32
-GROUPS = (('p', 0, 1), ('p', 1, 1), ('p', 2, 1), ('y', 3, 1), ('x', 4, 1), ('y', 5, 1), ('y', 6, 1), ('y', 7, 2), ('y', 9, 3))
+GROUPS = (('p', 0, 1), ('p', 1, 1), ('p', 2, 1), ('p', 3, 1), ('y', 4, 1), ('y', 5, 1), ('y', 6, 2), ('y', 8, 2), ('y', 10, 2))
 ORDER = (
-    ("x2p", 0), ("zy", 3), ("x2p", 1), ("zx", 4), ("zy", 5), ("x2p", 2),
-    ("yx", 3), ("x2x", 4), ("zp", 0), ("zy", 6), ("zp", 1), ("zp", 2),
-    ("zy", 7), ("yx", 5), ("yx", 6), ("y1", 4), ("x2y", 3), ("x2y", 5),
-    ("yx", 7), ("zy", 8), ("y1", 0), ("x2y", 6), ("yx", 8), ("x2y", 7),
-    ("ex", 4), ("ey", 5), ("y1", 1), ("y1", 2), ("x2y", 8), ("ey", 7),
-    ("ey", 3), ("ex", 0), ("ex", 2), ("ey", 6), ("ex", 1), ("ey", 8),
+    ("x2p", 0), ("zy", 4), ("x2p", 1), ("zy", 5), ("x2p", 2), ("x2p", 3),
+    ("yx", 4), ("zp", 0), ("zy", 6), ("zp", 1), ("yx", 5), ("zp", 2),
+    ("zp", 3), ("zy", 7), ("x2y", 4), ("yx", 6), ("zy", 8), ("x2y", 5),
+    ("yx", 7), ("yx", 8), ("y1", 0), ("x2y", 6), ("y1", 1), ("x2y", 7),
+    ("y1", 2), ("x2y", 8), ("y1", 3), ("ey", 4), ("ey", 5), ("ex", 0),
+    ("ex", 1), ("ey", 6), ("ex", 2), ("ey", 7), ("ey", 8), ("ex", 3),
 )
 MESH = pl.DeviceIdType.MESH
 
@@ -314,7 +314,7 @@
         pltpu.make_async_copy(out_ref.at[f], out_hbm.at[f], out_sem.at[f]).start()
         return carry
 
-    lax.fori_loop(0, BINS, one_bin, 0)
+    lax.fori_loop(0, BINS, one_bin, 0, unroll=6)
     for f in range(BINS):
         pltpu.make_async_copy(out_ref.at[f], out_hbm.at[f], out_sem.at[f]).wait()
 

time: 67 us -> 64.5 us (0.963)
  Pallas kernels: 66.1 us -> 63.9 us
    pallas_call x1, Pallas kernels: 5.07 us -> 3.12 us  [stacked(): pl.pallas_call(stack_kernel, out_shape=jax.ShapeDtypeStruct((BINS, 2, LAN...]
where the time goes in v6:
time: 64.5 us; the launch traced here: 63.9 us
  Pallas kernels  63.9 us (99%)
    pallas_call x1, Pallas kernels, gathered_spectra(): pl.pallas_call(gather_kernel, out_shape=jax.ShapeDtypeStruct((2, X_SIZE,...  60.8 us
    pallas_call x1, Pallas kernels, stacked(): pl.pallas_call(stack_kernel, out_shape=jax.ShapeDtypeStruct((BINS, 2, LAN...  3.12 us

profile of v6, /device:TPU:32, one launch (start us, length us, event | category | flops | bytes accessed | tf_op | source)
XLA Modules:
  0.0 63.9 jit_solution(5794562718587836166)
XLA Ops:
  0.0 60.8 %gather.1 = bf16[2,4,12,32,8,128]{5,4,3,2,1,0:T(8,128)(2,1)S(1)} custom-call(s32[4]{0:T(128)} %off_hbm.1, s32[4,128]{1,0:T(4,128)} %quality_hbm.1, f32[4,384,128]{2,1,0:T(8,128)} %constant.2.clone.seeds_hbm, bf16[4,3200,128]{2,1,0:T(8,128)(2,1)} %raw_hbm.1), custom_call_target="tpu_custom_call" | custom-call | tf_op jit(solution)/shard_map/gather/pallas_call | solution.py:265
  60.8 3.1 %stack.1 = bf16[12,2,128,1024]{3,2,1,0:T(8,128)(2,1)} custom-call(bf16[8,12,256,128]{3,2,1,0:T(8,128)(2,1)S(1)} %bitcast.1), custom_call_target="tpu_custom_call" | custom-call | tf_op jit(solution)/shard_map/stack/pallas_call | solution.py:323

commit v7 on v6

--- a/solution.py
+++ b/solution.py
@@ -22,14 +22,14 @@
 X_SIZE, Y_SIZE, Z_SIZE = 4, 4, 8
 COLUMN = 2 * Z_SIZE
 CHAN, WIN = 8, 32
-GROUPS = (('p', 0, 1), ('p', 1, 1), ('p', 2, 1), ('p', 3, 1), ('y', 4, 1), ('y', 5, 1), ('y', 6, 2), ('y', 8, 2), ('y', 10, 2))
+GROUPS = (('p', 0, 1), ('p', 1, 1), ('p', 2, 1), ('p', 3, 1), ('y', 4, 1), ('y', 5, 2), ('y', 7, 3), ('y', 10, 2))
 ORDER = (
-    ("x2p", 0), ("zy", 4), ("x2p", 1), ("zy", 5), ("x2p", 2), ("x2p", 3),
-    ("yx", 4), ("zp", 0), ("zy", 6), ("zp", 1), ("yx", 5), ("zp", 2),
-    ("zp", 3), ("zy", 7), ("x2y", 4), ("yx", 6), ("zy", 8), ("x2y", 5),
-    ("yx", 7), ("yx", 8), ("y1", 0), ("x2y", 6), ("y1", 1), ("x2y", 7),
-    ("y1", 2), ("x2y", 8), ("y1", 3), ("ey", 4), ("ey", 5), ("ex", 0),
-    ("ex", 1), ("ey", 6), ("ex", 2), ("ey", 7), ("ey", 8), ("ex", 3),
+    ("x2p", 0), ("zy", 4), ("x2p", 1), ("x2p", 2), ("zy", 5), ("x2p", 3),
+    ("yx", 4), ("zp", 0), ("zp", 1), ("zp", 2), ("zp", 3), ("zy", 6),
+    ("yx", 5), ("x2y", 4), ("zy", 7), ("yx", 6), ("x2y", 5), ("y1", 0),
+    ("yx", 7), ("y1", 1), ("x2y", 6), ("y1", 2), ("y1", 3), ("x2y", 7),
+    ("ey", 4), ("ex", 0), ("ey", 5), ("ex", 1), ("ex", 2), ("ey", 6),
+    ("ey", 7), ("ex", 3),
 )
 MESH = pl.DeviceIdType.MESH
 

time: 64.5 us -> 64.2 us (level)
  no operation moved by 1% of the time
where the time goes in v7:
time: 64.2 us
  Pallas kernels  64.2 us (100%)
    pallas_call x1, Pallas kernels, gathered_spectra(): pl.pallas_call(gather_kernel, out_shape=jax.ShapeDtypeStruct((2, X_SIZE,...  61.1 us
    pallas_call x1, Pallas kernels, stacked(): pl.pallas_call(stack_kernel, out_shape=jax.ShapeDtypeStruct((BINS, 2, LAN...  3.13 us

profile of v7, /device:TPU:32, one launch (start us, length us, event | category | flops | bytes accessed | tf_op | source)
XLA Modules:
  0.0 64.2 jit_solution(5208252222800698376)
XLA Ops:
  0.0 61.1 %gather.1 = bf16[2,4,12,32,8,128]{5,4,3,2,1,0:T(8,128)(2,1)S(1)} custom-call(s32[4]{0:T(128)} %off_hbm.1, s32[4,128]{1,0:T(4,128)} %quality_hbm.1, f32[4,384,128]{2,1,0:T(8,128)} %constant.2.clone.seeds_hbm, bf16[4,3200,128]{2,1,0:T(8,128)(2,1)} %raw_hbm.1), custom_call_target="tpu_custom_call" | custom-call | tf_op jit(solution)/shard_map/gather/pallas_call | solution.py:265
  61.1 3.1 %stack.1 = bf16[12,2,128,1024]{3,2,1,0:T(8,128)(2,1)} custom-call(bf16[8,12,256,128]{3,2,1,0:T(8,128)(2,1)S(1)} %bitcast.1), custom_call_target="tpu_custom_call" | custom-call | tf_op jit(solution)/shard_map/stack/pallas_call | solution.py:323
